TPU v7x, 32 devices: a whole 2x2x4 slice. The times are simulated.
32 devices in a mesh: groups: 2 (over y), ctx: 16 (over z, x, core).
Axes of the slice: x: 2, y: 2, z: 4, core: 2. Of those that a mesh axis runs over, the one named last changes fastest.
Arguments:
- queries: bfloat16 [4096, 4096], P(('groups', 'ctx')), parts along dimension 0, may hold values from -12 to 12
- context_keys: bfloat16 [32, 2048, 512], P('groups', 'ctx'), parts along dimension 0, may hold values from -6 to 6
- context_values: bfloat16 [32, 2048, 512], P('groups', 'ctx'), parts along dimension 0, may hold values from -6 to 6
- forward_output: bfloat16 [4096, 4096], P(('groups', 'ctx')), parts along dimension 0, may hold values from -6 to 6
- output_cotangent: bfloat16 [4096, 4096], P(('groups', 'ctx')), parts along dimension 0, may hold values from -48 to 48
- verticals: int32 [8, 8], P('groups'), parts along dimension 0, may hold values from 0 to 511, as said below
- offsets: int32 [8, 3], P('groups'), parts along dimension 0, may hold values from 1 to 10, as said below
- slab_index: int32 [2], P('groups'), parts along dimension 0, may hold values from 1 to 15
Outputs:
- query_grad: bfloat16 [4096, 4096], P(('groups', 'ctx')), parts along dimension 0
- key_gradient: bfloat16 [32, 2048, 512], P('groups', 'ctx'), parts along dimension 0
- value_gradient: bfloat16 [32, 2048, 512], P('groups', 'ctx'), parts along dimension 0
There are 2 independent parts, one for each index of `groups`. A program takes and returns all parts, laid end to end along the dimension named above; each array names one. Nothing has to cross between parts.
Inputs may be any that keep to these rules, and one draw needn't show every extreme that they name: `verticals`: each row holds 8 distinct block numbers; the first of every row is 0, and some row names the last block. Each row holds 3 distinct offsets; some row names 10.
All inputs are finite; a program needn't handle non-finite values.
Results may differ from a plain program's by a relative error of at most 0.0051.
Values may be sent and summed in bfloat16 or wider, within the bound.
A program may use at most 128 MiB of HBM per device.

v0:
```python
import math

import jax
import jax.numpy as jnp
from jax import lax
from jax.sharding import PartitionSpec as P

MASK_BLOCK_SIZE = 64
WDEV = 5
NV = 8
SLASH_COUNT = 3


def from_behind(shard, axis, by):
    peers = lax.axis_size(axis)
    return lax.ppermute(shard, axis, [(i, (i + by) % peers) for i in range(peers)])


def pick_region(stack, which_region):
    return lax.dynamic_index_in_dim(stack, which_region, 0, keepdims=False)


def head_pass(inputs):
    q_head, grad_head, delta_head, keys_cand, values_cand, visible = inputs
    scaling = 1.0 / math.sqrt(q_head.shape[-1])
    scores = (
        jnp.einsum("jrgd,jkd->jrgk", q_head, keys_cand, preferred_element_type=jnp.float32)
        * scaling
    )
    masked = jnp.where(visible[:, :, None, :], scores, -jnp.inf)
    row_max = jnp.max(masked, axis=-1, keepdims=True)
    row_sum = jnp.sum(jnp.exp(masked - row_max), axis=-1, keepdims=True)
    weights = jnp.exp(masked - (row_max + jnp.log(row_sum)))
    weight_grad = jnp.einsum(
        "jrgd,jkd->jrgk", grad_head, values_cand, preferred_element_type=jnp.float32
    )
    score_grad = weights * (weight_grad - delta_head[..., None])
    weights_low = weights.astype(jnp.bfloat16)
    score_low = score_grad.astype(jnp.bfloat16)
    value_part = jnp.einsum(
        "jrgk,jrgd->jkd", weights_low, grad_head, preferred_element_type=jnp.float32
    )
    key_part = (
        jnp.einsum("jrgk,jrgd->jkd", score_low, q_head, preferred_element_type=jnp.float32)
        * scaling
    )
    query_part = (
        jnp.einsum("jrgk,jkd->jrgd", score_low, keys_cand, preferred_element_type=jnp.float32)
        * scaling
    )
    return (query_part, key_part, value_part)


def shards(
    queries,
    context_keys,
    context_values,
    forward_output,
    output_cotangent,
    verticals,
    offsets,
    slab_index,
):
    devices = lax.axis_size("ctx")
    my_index = lax.axis_index("ctx")
    row_count = queries.shape[0]
    regions = context_keys.shape[0]
    heads_kv = verticals.shape[0]
    features = context_keys.shape[2]
    head_dim = features // heads_kv
    query_per_key_head = queries.shape[1] // features
    per_device = row_count // MASK_BLOCK_SIZE
    blocks_per_slab = per_device * devices
    local_blocks = regions * per_device
    window_blocks = (WDEV + 1) * per_device
    cand_count = 1 + NV + SLASH_COUNT
    present_slab = slab_index[0]
    first_block = present_slab * blocks_per_slab + my_index * per_device
    slab_local_keys = pick_region(context_keys, present_slab)
    own_values = pick_region(context_values, present_slab)
    prior_keys = pick_region(context_keys, present_slab - 1)
    prior_values = pick_region(context_values, present_slab - 1)
    head_numbers = jnp.arange(heads_kv, dtype=jnp.int32)[:, None]
    arrived = []
    for distance in range(1, WDEV + 1):
        wrapped = my_index + distance >= devices
        send_keys = jnp.where(wrapped, prior_keys, slab_local_keys)
        send_values = jnp.where(wrapped, prior_values, own_values)
        arrived.append(from_behind((send_keys, send_values), "ctx", distance))
    window_keys = jnp.concatenate(
        [received[0] for received in reversed(arrived)] + [slab_local_keys], axis=0
    )
    window_values = jnp.concatenate(
        [received[1] for received in reversed(arrived)] + [own_values], axis=0
    )
    window_keys = window_keys.reshape(window_blocks, MASK_BLOCK_SIZE, heads_kv, head_dim)
    window_values = window_values.reshape(window_blocks, MASK_BLOCK_SIZE, heads_kv, head_dim)
    vert_region = verticals // blocks_per_slab
    vert_inner = verticals % blocks_per_slab
    vert_owner = vert_inner // per_device
    vert_local = vert_region * per_device + vert_inner % per_device
    owned_view = (vert_owner == my_index)[:, :, None, None]
    local_keys = context_keys.reshape(local_blocks, MASK_BLOCK_SIZE, heads_kv, head_dim)
    local_values = context_values.reshape(local_blocks, MASK_BLOCK_SIZE, heads_kv, head_dim)
    picked_keys = jnp.where(
        owned_view, local_keys[vert_local, :, head_numbers].astype(jnp.float32), 0.0
    )
    picked_values = jnp.where(
        owned_view, local_values[vert_local, :, head_numbers].astype(jnp.float32), 0.0
    )
    vert_keys, vert_values = lax.psum((picked_keys, picked_values), "ctx")
    vert_keys = vert_keys.astype(jnp.bfloat16)
    vert_values = vert_values.astype(jnp.bfloat16)
    query_blocks = first_block + jnp.arange(per_device, dtype=jnp.int32)
    slash_blocks = query_blocks[None, :, None] - offsets[:, None, :]
    collide = jnp.any(slash_blocks[..., None] == verticals[:, None, None, :], axis=-1)
    slash_valid = (offsets[:, None, :] > 0) & jnp.logical_not(collide)
    vertical_valid = verticals[:, None, :] < query_blocks[None, :, None]
    window_at = WDEV * per_device + jnp.arange(per_device, dtype=jnp.int32)
    local_at = jnp.concatenate(
        [
            jnp.broadcast_to(window_at[None, :, None], (heads_kv, per_device, 1)),
            window_at[None, :, None] - offsets[:, None, :],
        ],
        axis=-1,
    )
    head_grid = head_numbers[:, :, None]
    near_keys = window_keys[local_at, :, head_grid]
    near_values = window_values[local_at, :, head_grid]
    vert_shape = (heads_kv, per_device, NV, MASK_BLOCK_SIZE, head_dim)
    cand_keys = jnp.concatenate(
        [
            near_keys[:, :, :1],
            jnp.broadcast_to(vert_keys[:, None], vert_shape),
            near_keys[:, :, 1:],
        ],
        axis=2,
    )
    cand_values = jnp.concatenate(
        [
            near_values[:, :, :1],
            jnp.broadcast_to(vert_values[:, None], vert_shape),
            near_values[:, :, 1:],
        ],
        axis=2,
    )
    cand_blocks = jnp.concatenate(
        [
            jnp.broadcast_to(query_blocks[None, :, None], (heads_kv, per_device, 1)),
            jnp.broadcast_to(verticals[:, None, :], (heads_kv, per_device, NV)),
            slash_blocks,
        ],
        axis=-1,
    )
    candidate_valid = jnp.concatenate(
        [jnp.ones((heads_kv, per_device, 1), jnp.bool_), vertical_valid, slash_valid], axis=-1
    )
    lower_tri = jnp.arange(MASK_BLOCK_SIZE)[:, None] >= jnp.arange(MASK_BLOCK_SIZE)[None, :]
    causal = (cand_blocks < query_blocks[None, :, None])[..., None, None] | lower_tri[
        None, None, None
    ]
    visible = (
        (candidate_valid[..., None, None] & causal)
        .transpose(0, 1, 3, 2, 4)
        .reshape(heads_kv, per_device, MASK_BLOCK_SIZE, cand_count * MASK_BLOCK_SIZE)
    )
    q_heads = queries.reshape(
        per_device, MASK_BLOCK_SIZE, heads_kv, query_per_key_head, head_dim
    ).transpose(2, 0, 1, 3, 4)
    grad_heads = output_cotangent.reshape(
        per_device, MASK_BLOCK_SIZE, heads_kv, query_per_key_head, head_dim
    ).transpose(2, 0, 1, 3, 4)
    products = output_cotangent.astype(jnp.float32) * forward_output.astype(jnp.float32)
    delta_rows = jnp.sum(
        products.reshape(per_device, MASK_BLOCK_SIZE, heads_kv, query_per_key_head, head_dim),
        axis=-1,
    )
    delta_heads = delta_rows.transpose(2, 0, 1, 3)
    flat_keys = cand_keys.reshape(heads_kv, per_device, cand_count * MASK_BLOCK_SIZE, head_dim)
    flat_values = cand_values.reshape(heads_kv, per_device, cand_count * MASK_BLOCK_SIZE, head_dim)
    query_part, key_part, value_part = lax.map(
        head_pass, (q_heads, grad_heads, delta_heads, flat_keys, flat_values, visible)
    )
    query_grad = (
        query_part.transpose(1, 2, 0, 3, 4)
        .reshape(row_count, heads_kv * query_per_key_head * head_dim)
        .astype(jnp.bfloat16)
    )
    key_part = key_part.reshape(heads_kv, per_device, cand_count, MASK_BLOCK_SIZE, head_dim)
    value_part = value_part.reshape(heads_kv, per_device, cand_count, MASK_BLOCK_SIZE, head_dim)
    near_key_part = jnp.concatenate([key_part[:, :, :1], key_part[:, :, 1 + NV :]], axis=2)
    near_value_part = jnp.concatenate([value_part[:, :, :1], value_part[:, :, 1 + NV :]], axis=2)
    blank_window = jnp.zeros((window_blocks, MASK_BLOCK_SIZE, heads_kv, head_dim), jnp.float32)
    near_key_flat = (
        blank_window.at[local_at, :, head_grid]
        .add(near_key_part)
        .reshape(window_blocks * MASK_BLOCK_SIZE, features)
    )
    near_value_flat = (
        blank_window.at[local_at, :, head_grid]
        .add(near_value_part)
        .reshape(window_blocks * MASK_BLOCK_SIZE, features)
    )

    def portion(flat_rows, distance):
        lower_row = (WDEV - distance) * row_count
        return flat_rows[lower_row : lower_row + row_count]

    home_keys = near_key_flat[WDEV * row_count :]
    home_values = near_value_flat[WDEV * row_count :]
    prior_key_sum = jnp.zeros((row_count, features), jnp.float32)
    prior_value_sum = jnp.zeros((row_count, features), jnp.float32)
    for distance in range(1, WDEV + 1):
        back_keys, back_values = from_behind(
            (portion(near_key_flat, distance), portion(near_value_flat, distance)), "ctx", -distance
        )
        wrapped = my_index + distance >= devices
        home_keys = home_keys + jnp.where(wrapped, 0.0, back_keys)
        home_values = home_values + jnp.where(wrapped, 0.0, back_values)
        prior_key_sum = prior_key_sum + jnp.where(wrapped, back_keys, 0.0)
        prior_value_sum = prior_value_sum + jnp.where(wrapped, back_values, 0.0)
    vert_key_grad, vert_value_grad = lax.psum(
        (
            jnp.sum(key_part[:, :, 1 : 1 + NV], axis=1),
            jnp.sum(value_part[:, :, 1 : 1 + NV], axis=1),
        ),
        "ctx",
    )
    blank_local = jnp.zeros((local_blocks, MASK_BLOCK_SIZE, heads_kv, head_dim), jnp.float32)
    owned_keys = (
        blank_local.at[vert_local, :, head_numbers]
        .add(jnp.where(owned_view, vert_key_grad, 0.0))
        .reshape(regions, row_count, features)
    )
    owned_values = (
        blank_local.at[vert_local, :, head_numbers]
        .add(jnp.where(owned_view, vert_value_grad, 0.0))
        .reshape(regions, row_count, features)
    )
    region_ids = jnp.arange(regions)[:, None, None]
    key_total = (
        owned_keys
        + jnp.where(region_ids == present_slab, home_keys[None], 0.0)
        + jnp.where(region_ids == present_slab - 1, prior_key_sum[None], 0.0)
    )
    value_total = (
        owned_values
        + jnp.where(region_ids == present_slab, home_values[None], 0.0)
        + jnp.where(region_ids == present_slab - 1, prior_value_sum[None], 0.0)
    )
    return (query_grad, key_total.astype(jnp.bfloat16), value_total.astype(jnp.bfloat16))


def solution(mesh):
    in_specs = (
        P(("groups", "ctx"), None),
        P("groups", "ctx", None),
        P("groups", "ctx", None),
        P(("groups", "ctx"), None),
        P(("groups", "ctx"), None),
        P("groups", None),
        P("groups", None),
        P("groups"),
    )
    out_specs = (P(("groups", "ctx"), None), P("groups", "ctx", None), P("groups", "ctx", None))
    return jax.shard_map(shards, mesh=mesh, in_specs=in_specs, out_specs=out_specs, check_vma=False)
```

profile of v0, /device:TPU:25, one launch (start us, length us, event | category | flops | bytes accessed | tf_op | source)
XLA Modules:
  0.0 410.9 jit_solution(1168465586102998522)
XLA Ops:
  7.9 1.9 bitcast_select_fusion
  9.8 1.4 collective-permute-start.5
  11.2 1.3 collective-permute-start.6
  14.1 2.7 collective-permute-start.9
  18.8 2.5 reshape.192
  21.4 4.0 reshape.188
  25.3 2.0 bitcast_select_fusion.5
  27.8 3.5 copy.119
  31.2 1.9 copy.121
  33.1 3.0 gather_fusion.1
  36.1 3.1 gather_fusion.3
  39.3 1.4 convert_select_fusion
  44.6 69.7 %all-reduce.6 = (bf16[4,8,64,128]{3,2,1,0:T(8,128)(2,1)}, bf16[4,8,64,128]{3,2,1,0:T(8,128)(2,1)}) all-reduce(f32[4,8,64,128]{3,2,1,0:T(8,128)S(1)} %get-tuple-element.163, f32[4,8,64,128]{3,2,1,0:T(8,128)S(1)} %get-tuple-element.162), channel_id=1, replica_groups=mesh['groups'=2,'ctx'=16] {'ctx'}, use_global_device_ids=true, to_apply=%region_1.2 | all-reduce | flops 524288 | bytes 3145728 | tf_op jit(solution)/shard_map/psum | solution.py:111
  114.3 2.8 multiply_bitcast_fusion
  118.6 2.1 copy.150
  120.6 1.4 copy.148
  124.2 1.5 reduce_sum.36
  125.8 3.4 collective-permute-start
  131.1 3.4 collective-permute-start.2
  136.4 1.7 collective-permute-start.4
  144.5 1.6 constant_dynamic-update-slice_fusion.1
  146.0 1.6 constant_dynamic-update-slice_fusion
  147.6 1.6 bitcast_dynamic-update-slice_fusion.1
  149.2 1.7 reshape.187
  151.9 1.3 broadcast_in_dim.232
  153.2 2.3 pad_maximum_fusion.1
  156.1 42.9 %while.14 = (s32[]{:T(128)}, bf16[4,2,64,8,128]{4,3,2,1,0:T(8,128)(2,1)}, f32[4,2,768,128]{3,2,1,0:T(8,128)}, f32[4,2,768,128]{3,2,1,0:T(8,128)}, pred[4,2,64,76...) while((s32[]{:T(128)}, ...), condition=%wide.region_7.8_spmd, body=%wide.region_4.7_spmd.sunk | while | flops 1020328960 | bytes 26645648 | solution.py:181
  158.2 2.3 fusion.88
  161.5 2.4 multiply_convert_fusion.2
  163.9 1.6 fusion.87
  168.9 2.3 fusion.88
  172.2 2.4 multiply_convert_fusion.2
  174.6 1.7 fusion.87
  176.3 1.3 fusion.86
  179.6 2.3 fusion.88
  183.0 2.4 multiply_convert_fusion.2
  185.4 1.6 fusion.87
  187.0 1.3 fusion.86
  190.3 2.3 fusion.88
  193.7 2.4 multiply_convert_fusion.2
  196.1 1.6 fusion.87
  199.0 1.3 slice.158
  201.3 2.8 slice_reduce_fusion.1
  205.6 2.4 scatter_fusion.1
  212.1 4.9 %collective-permute-start.11 = (f32[128,512]{1,0:T(8,128)}, f32[128,512]{1,0:T(8,128)}, u32[]{:S(2)}, u32[]{:S(2)}) collective-permute-start(f32[128,512]{1,0:T(8,128)} %bitcast.217), channel_id=1, source_target_pairs={{0,14},{1,15},{2,0},{3,1},{4,2},{5,3},{6,4},{7,5},{8,6},{9,7},{10,... | collective-permute-start | bytes 786440 | tf_op jit(solution)/shard_map/ppermute | solution.py:16
  220.7 3.3 collective-permute-start.14
  224.4 2.4 scatter_fusion.3
  228.9 1.4 copy.125
  232.4 1.9 collective-permute-start.16
  234.3 13.3 %collective-permute-done.12 = f32[128,512]{1,0:T(8,128)} collective-permute-done((f32[128,512]{1,0:T(8,128)}, f32[128,512]{1,0:T(8,128)}, u32[]{:S(2)}, u32[]{:S(2)}) %collective-permute-start.12) | collective-permute-done | bytes 262176 | tf_op jit(solution)/shard_map/ppermute | solution.py:16
  249.8 8.0 %collective-permute-start.19 = (f32[128,512]{1,0:T(8,128)}, f32[128,512]{1,0:T(8,128)S(1)}, u32[]{:S(2)}, u32[]{:S(2)}) collective-permute-start(f32[128,512]{1,0:T(8,128)} %bitcast.209), channel_id=1, source_target_pairs={{0,11},{1,12},{2,13},{3,14},{4,15},{5,0},{6,1},{7,2},{8,3},{9,4},{... | collective-permute-start | bytes 786440 | tf_op jit(solution)/shard_map/ppermute | solution.py:16
  257.8 1.5 fusion.48
  259.3 17.1 %collective-permute-done.17 = f32[128,512]{1,0:T(8,128)S(1)} collective-permute-done((f32[128,512]{1,0:T(8,128)S(1)}, f32[128,512]{1,0:T(8,128)S(1)}, u32[]{:S(2)}, u32[]{:S(2)}) %collective-permute-start.17) | collective-permute-done | bytes 262176 | tf_op jit(solution)/shard_map/ppermute | solution.py:16
  276.7 76.6 %all-reduce.5.cloned.1.call-done = (f32[4,8,64,128]{3,2,1,0:T(8,128)}, f32[4,8,64,128]{3,2,1,0:T(8,128)}) async-done(((f32[4,8,64,128]{3,2,1,0:T(8,128)}, f32[4,8,64,128]{3,2,1,0:T(8,128)}), (f32[4,8,64,128]{3,2,1,0:T(8,128)}, f32[4,8,64,128]{3,2,1,0:T(8,128)})) %all-reduce.5.cloned.1.call-update) | async-done | bytes 2097168 | tf_op jit(solution)/shard_map/psum | solution.py:222
  353.2 1.7 broadcast_select_fusion
  355.0 2.5 broadcast_in_dim.233.clone.1
  357.5 5.2 %scatter_fusion = f32[32,64,4,128]{3,1,2,0:T(8,128)} fusion(f32[32,64,4,128]{3,1,2,0:T(8,128)} %broadcast_in_dim.233.clone.1, s32[32]{0:T(128)S(1)} %reshape.223, f32[32,64,128]{2,1,0:T(8,128)S(1)} %bitcast.260), kind=kCustom, calls=%fused_computation.4 | custom fusion | flops 262144 | bytes 3145984 | tf_op jit(solution)/shard_map/scatter-add | solution.py:232
  362.6 7.8 %copy.126 = f32[32,64,4,128]{3,2,1,0:T(4,128)} copy(f32[32,64,4,128]{3,1,2,0:T(8,128)} %scatter_fusion) | data formatting | bytes 8388608 | tf_op jit(solution)/shard_map/scatter-add | solution.py:232
  370.4 5.5 %reshape.196 = f32[16,128,512]{2,1,0:T(8,128)} reshape(f32[32,64,4,128]{3,2,1,0:T(4,128)} %copy.126) | data formatting | bytes 8388608 | tf_op jit(solution)/shard_map/reshape | solution.py:233
  375.9 2.5 broadcast_in_dim.233.clone
  378.4 5.2 %scatter_fusion.2 = f32[32,64,4,128]{3,1,2,0:T(8,128)} fusion(f32[32,64,4,128]{3,1,2,0:T(8,128)} %broadcast_in_dim.233.clone, s32[32]{0:T(128)S(1)} %reshape.223, f32[32,64,128]{2,1,0:T(8,128)S(1)} %bitcast.259), kind=kCustom, calls=%fused_computation.6 | custom fusion | flops 262144 | bytes 3145984 | tf_op jit(solution)/shard_map/scatter-add | solution.py:237
  383.5 7.8 %copy.134 = f32[32,64,4,128]{3,2,1,0:T(4,128)} copy(f32[32,64,4,128]{3,1,2,0:T(8,128)} %scatter_fusion.2) | data formatting | bytes 8388608 | tf_op jit(solution)/shard_map/scatter-add | solution.py:237
  391.3 5.5 %reshape.198 = f32[16,128,512]{2,1,0:T(8,128)} reshape(f32[32,64,4,128]{3,2,1,0:T(4,128)} %copy.134) | data formatting | bytes 8388608 | tf_op jit(solution)/shard_map/reshape | solution.py:238
  396.8 7.2 %add_convert_fusion = (bf16[16,128,512]{2,1,0:T(8,128)(2,1)}, bf16[16,128,512]{2,1,0:T(8,128)(2,1)}) fusion(f32[16,128,512]{2,1,0:T(8,128)} %reshape.198, f32[128,512]{1,0:T(8,128)S(1)} %get-tuple-element.153, f32[128,512]{1,0:T(8,128)S(1)} %get-tuple-element.152, pred[16]{0:T(512)(128)(4,1)S(1)} %copy-done.13, pred[16]{0:T(512)(128)(4,1)S(1)} %copy-done.14, ...), kind=kLoop, calls=%fused_computation.53 | loop fusion | flops 10485760 | bytes 13631520 | tf_op jit(solution)/shard_map/convert_element_type | solution.py:251
  (185 shorter events, 55.0 us)
Async XLA Ops:
  7.2 346.1 %all-reduce.5.cloned.1.call-start = ((), (), s32[]{:S(2)}) async-start(), calls=%async_computation | async-start | bytes 4194304 | tf_op jit(solution)/shard_map/psum | solution.py:222
  9.8 116.0 %collective-permute-start.5 = (bf16[128,512]{1,0:T(8,128)(2,1)}, bf16[128,512]{1,0:T(8,128)(2,1)}, u32[]{:S(2)}, u32[]{:S(2)}) collective-permute-start(bf16[128,512]{1,0:T(8,128)(2,1)} %get-tuple-element.134), channel_id=1, source_target_pairs={{0,5},{1,6},{2,7},{3,8},{4,9},{5,10},{6,11},{7,12},{8,13},{9,14},{... | collective-permute-start | bytes 393224 | tf_op jit(solution)/shard_map/ppermute | solution.py:16
  11.2 118.9 %collective-permute-start.6 = (bf16[128,512]{1,0:T(8,128)(2,1)}, bf16[128,512]{1,0:T(8,128)(2,1)}, u32[]{:S(2)}, u32[]{:S(2)}) collective-permute-start(bf16[128,512]{1,0:T(8,128)(2,1)} %get-tuple-element.133), channel_id=1, source_target_pairs={{0,4},{1,5},{2,6},{3,7},{4,8},{5,9},{6,10},{7,11},{8,12},{9,13},{1... | collective-permute-start | bytes 393224 | tf_op jit(solution)/shard_map/ppermute | solution.py:16
  12.5 118.6 %collective-permute-start.7 = (bf16[128,512]{1,0:T(8,128)(2,1)}, bf16[128,512]{1,0:T(8,128)(2,1)}, u32[]{:S(2)}, u32[]{:S(2)}) collective-permute-start(bf16[128,512]{1,0:T(8,128)(2,1)} %get-tuple-element.132), channel_id=1, source_target_pairs={{0,3},{1,4},{2,5},{3,6},{4,7},{5,8},{6,9},{7,10},{8,11},{9,12},{10... | collective-permute-start | bytes 393224 | tf_op jit(solution)/shard_map/ppermute | solution.py:16
  12.9 122.5 %collective-permute-start.8 = (bf16[128,512]{1,0:T(8,128)(2,1)}, bf16[128,512]{1,0:T(8,128)(2,1)}, u32[]{:S(2)}, u32[]{:S(2)}) collective-permute-start(bf16[128,512]{1,0:T(8,128)(2,1)} %get-tuple-element.131), channel_id=1, source_target_pairs={{0,2},{1,3},{2,4},{3,5},{4,6},{5,7},{6,8},{7,9},{8,10},{9,11},{10,... | collective-permute-start | bytes 393224 | tf_op jit(solution)/shard_map/ppermute | solution.py:16
  14.1 122.3 %collective-permute-start.9 = (bf16[128,512]{1,0:T(8,128)(2,1)}, bf16[128,512]{1,0:T(8,128)(2,1)}, u32[]{:S(2)}, u32[]{:S(2)}) collective-permute-start(bf16[128,512]{1,0:T(8,128)(2,1)} %get-tuple-element.130), channel_id=1, source_target_pairs={{0,1},{1,2},{2,3},{3,4},{4,5},{5,6},{6,7},{7,8},{8,9},{9,10},{10,1... | collective-permute-start | bytes 393224 | tf_op jit(solution)/shard_map/ppermute | solution.py:16
  17.5 21.8 %copy-start.11 = (pred[4,8]{1,0:T(4,128)(4,1)}, pred[4,8]{1,0:T(4,128)(4,1)S(1)}, u32[]{:S(2)}) copy-start(pred[4,8]{1,0:T(4,128)(4,1)S(1)} %fusion.53) | copy-start | bytes 100
  21.3 6.0 %copy-start.10 = (s32[4,3]{1,0:T(4,128)S(1)}, s32[4,3]{1,0:T(4,128)}, u32[]{:S(2)}) copy-start(s32[4,3]{1,0:T(4,128)} %param.16) | copy-start | bytes 148
  21.3 6.2 %copy-start.6 = (s32[4,8]{1,0:T(4,128)S(1)}, s32[4,8]{1,0:T(4,128)}, u32[]{:S(2)}) copy-start(s32[4,8]{1,0:T(4,128)} %param.15) | copy-start | bytes 388
  36.1 78.1 %copy-start = (bf16[128,4096]{1,0:T(8,128)(2,1)S(1)}, bf16[128,4096]{1,0:T(8,128)(2,1)}, u32[]{:S(2)}) copy-start(bf16[128,4096]{1,0:T(8,128)(2,1)} %param.14) | copy-start | bytes 3145732
  44.6 72.5 %copy-start.7 = (pred[4,2,768]{2,1,0:T(4,128)(4,1)S(1)}, pred[4,2,768]{2,1,0:T(4,128)(4,1)}, u32[]{:S(2)}) copy-start(pred[4,2,768]{2,1,0:T(4,128)(4,1)} %copy.116) | copy-start | bytes 18436
  114.3 2.8 copy-start.5
  114.3 2.8 copy-start.8
  114.3 4.1 %copy-start.9 = (s32[4,2,4,1]{0,1,3,2:T(2,128)S(1)}, s32[4,2,4,1]{0,1,3,2:T(2,128)}, u32[]{:S(2)}) copy-start(s32[4,2,4,1]{0,1,3,2:T(2,128)} %get-tuple-element.125) | copy-start | bytes 388
  118.6 3.5 copy-start.1
  125.8 14.2 %collective-permute-start = (bf16[128,512]{1,0:T(8,128)(2,1)}, bf16[128,512]{1,0:T(8,128)(2,1)S(1)}, u32[]{:S(2)}, u32[]{:S(2)}) collective-permute-start(bf16[128,512]{1,0:T(8,128)(2,1)} %get-tuple-element.139), channel_id=1, source_target_pairs={{0,5},{1,6},{2,7},{3,8},{4,9},{5,10},{6,11},{7,12},{8,13},{9,14},{... | collective-permute-start | bytes 393224 | tf_op jit(solution)/shard_map/ppermute | solution.py:16
  130.1 10.5 %collective-permute-start.1 = (bf16[128,512]{1,0:T(8,128)(2,1)}, bf16[128,512]{1,0:T(8,128)(2,1)S(1)}, u32[]{:S(2)}, u32[]{:S(2)}) collective-permute-start(bf16[128,512]{1,0:T(8,128)(2,1)} %get-tuple-element.138), channel_id=1, source_target_pairs={{0,4},{1,5},{2,6},{3,7},{4,8},{5,9},{6,10},{7,11},{8,12},{9,13},{1... | collective-permute-start | bytes 393224 | tf_op jit(solution)/shard_map/ppermute | solution.py:16
  131.1 10.2 %collective-permute-start.2 = (bf16[128,512]{1,0:T(8,128)(2,1)}, bf16[128,512]{1,0:T(8,128)(2,1)S(1)}, u32[]{:S(2)}, u32[]{:S(2)}) collective-permute-start(bf16[128,512]{1,0:T(8,128)(2,1)} %get-tuple-element.137), channel_id=1, source_target_pairs={{0,3},{1,4},{2,5},{3,6},{4,7},{5,8},{6,9},{7,10},{8,11},{9,12},{10... | collective-permute-start | bytes 393224 | tf_op jit(solution)/shard_map/ppermute | solution.py:16
  135.4 9.1 %collective-permute-start.3 = (bf16[128,512]{1,0:T(8,128)(2,1)}, bf16[128,512]{1,0:T(8,128)(2,1)}, u32[]{:S(2)}, u32[]{:S(2)}) collective-permute-start(bf16[128,512]{1,0:T(8,128)(2,1)} %get-tuple-element.136), channel_id=1, source_target_pairs={{0,2},{1,3},{2,4},{3,5},{4,6},{5,7},{6,8},{7,9},{8,10},{9,11},{10,... | collective-permute-start | bytes 393224 | tf_op jit(solution)/shard_map/ppermute | solution.py:16
  136.4 9.6 %collective-permute-start.4 = (bf16[128,512]{1,0:T(8,128)(2,1)}, bf16[128,512]{1,0:T(8,128)(2,1)}, u32[]{:S(2)}, u32[]{:S(2)}) collective-permute-start(bf16[128,512]{1,0:T(8,128)(2,1)} %get-tuple-element.135), channel_id=1, source_target_pairs={{0,1},{1,2},{2,3},{3,4},{4,5},{5,6},{6,7},{7,8},{8,9},{9,10},{10,1... | collective-permute-start | bytes 393224 | tf_op jit(solution)/shard_map/ppermute | solution.py:16
  151.8 3.7 copy-start.4
  156.1 2.0 copy-start.3
  166.8 2.0 copy-start.3
  177.6 2.1 copy-start.3
  188.3 2.1 copy-start.3
  199.0 5.1 %copy-start.2 = (f32[4,2,768,128]{3,2,1,0:T(8,128)S(1)}, f32[4,2,768,128]{3,2,1,0:T(8,128)}, u32[]{:S(2)}) copy-start(f32[4,2,768,128]{3,2,1,0:T(8,128)} %get-tuple-element.59) | copy-start | bytes 9437188
  211.3 20.4 %collective-permute-start.10 = (f32[128,512]{1,0:T(8,128)}, f32[128,512]{1,0:T(8,128)}, u32[]{:S(2)}, u32[]{:S(2)}) collective-permute-start(f32[128,512]{1,0:T(8,128)} %bitcast.218), channel_id=1, source_target_pairs={{0,15},{1,0},{2,1},{3,2},{4,3},{5,4},{6,5},{7,6},{8,7},{9,8},{10,9... | collective-permute-start | bytes 786440 | tf_op jit(solution)/shard_map/ppermute | solution.py:16
  212.1 20.2 %collective-permute-start.11 = (f32[128,512]{1,0:T(8,128)}, f32[128,512]{1,0:T(8,128)}, u32[]{:S(2)}, u32[]{:S(2)}) collective-permute-start(f32[128,512]{1,0:T(8,128)} %bitcast.217), channel_id=1, source_target_pairs={{0,14},{1,15},{2,0},{3,1},{4,2},{5,3},{6,4},{7,5},{8,6},{9,7},{10,... | collective-permute-start | bytes 786440 | tf_op jit(solution)/shard_map/ppermute | solution.py:16
  217.9 29.6 %collective-permute-start.12 = (f32[128,512]{1,0:T(8,128)}, f32[128,512]{1,0:T(8,128)}, u32[]{:S(2)}, u32[]{:S(2)}) collective-permute-start(f32[128,512]{1,0:T(8,128)} %bitcast.216), channel_id=1, source_target_pairs={{0,13},{1,14},{2,15},{3,0},{4,1},{5,2},{6,3},{7,4},{8,5},{9,6},{10... | collective-permute-start | bytes 786440 | tf_op jit(solution)/shard_map/ppermute | solution.py:16
  218.8 29.8 %collective-permute-start.13 = (f32[128,512]{1,0:T(8,128)}, f32[128,512]{1,0:T(8,128)}, u32[]{:S(2)}, u32[]{:S(2)}) collective-permute-start(f32[128,512]{1,0:T(8,128)} %bitcast.215), channel_id=1, source_target_pairs={{0,12},{1,13},{2,14},{3,15},{4,0},{5,1},{6,2},{7,3},{8,4},{9,5},{1... | collective-permute-start | bytes 786440 | tf_op jit(solution)/shard_map/ppermute | solution.py:16
  220.7 29.1 %collective-permute-start.14 = (f32[128,512]{1,0:T(8,128)}, f32[128,512]{1,0:T(8,128)}, u32[]{:S(2)}, u32[]{:S(2)}) collective-permute-start(f32[128,512]{1,0:T(8,128)} %bitcast.214), channel_id=1, source_target_pairs={{0,11},{1,12},{2,13},{3,14},{4,15},{5,0},{6,1},{7,2},{8,3},{9,4},{... | collective-permute-start | bytes 786440 | tf_op jit(solution)/shard_map/ppermute | solution.py:16
  230.3 122.9 %copy-start.12 = (pred[4,8]{1,0:T(4,128)(4,1)S(1)}, pred[4,8]{1,0:T(4,128)(4,1)}, u32[]{:S(2)}) copy-start(pred[4,8]{1,0:T(4,128)(4,1)} %copy-done.11) | copy-start | bytes 100
  231.6 27.7 %collective-permute-start.15 = (f32[128,512]{1,0:T(8,128)S(1)}, f32[128,512]{1,0:T(8,128)S(1)}, u32[]{:S(2)}, u32[]{:S(2)}) collective-permute-start(f32[128,512]{1,0:T(8,128)S(1)} %bitcast.290), channel_id=1, source_target_pairs={{0,15},{1,0},{2,1},{3,2},{4,3},{5,4},{6,5},{7,6},{8,7},{9,8},{10,9... | collective-permute-start | bytes 786440 | tf_op jit(solution)/shard_map/ppermute | solution.py:16
  232.4 27.0 %collective-permute-start.16 = (f32[128,512]{1,0:T(8,128)S(1)}, f32[128,512]{1,0:T(8,128)S(1)}, u32[]{:S(2)}, u32[]{:S(2)}) collective-permute-start(f32[128,512]{1,0:T(8,128)S(1)} %bitcast.291), channel_id=1, source_target_pairs={{0,14},{1,15},{2,0},{3,1},{4,2},{5,3},{6,4},{7,5},{8,6},{9,7},{10,... | collective-permute-start | bytes 786440 | tf_op jit(solution)/shard_map/ppermute | solution.py:16
  247.5 29.0 %collective-permute-start.17 = (f32[128,512]{1,0:T(8,128)S(1)}, f32[128,512]{1,0:T(8,128)S(1)}, u32[]{:S(2)}, u32[]{:S(2)}) collective-permute-start(f32[128,512]{1,0:T(8,128)S(1)} %bitcast.292), channel_id=1, source_target_pairs={{0,13},{1,14},{2,15},{3,0},{4,1},{5,2},{6,3},{7,4},{8,5},{9,6},{10... | collective-permute-start | bytes 786440 | tf_op jit(solution)/shard_map/ppermute | solution.py:16
  248.6 27.9 %collective-permute-start.18 = (f32[128,512]{1,0:T(8,128)S(1)}, f32[128,512]{1,0:T(8,128)S(1)}, u32[]{:S(2)}, u32[]{:S(2)}) collective-permute-start(f32[128,512]{1,0:T(8,128)S(1)} %bitcast.293), channel_id=1, source_target_pairs={{0,12},{1,13},{2,14},{3,15},{4,0},{5,1},{6,2},{7,3},{8,4},{9,5},{1... | collective-permute-start | bytes 786440 | tf_op jit(solution)/shard_map/ppermute | solution.py:16
  249.8 26.6 %collective-permute-start.19 = (f32[128,512]{1,0:T(8,128)}, f32[128,512]{1,0:T(8,128)S(1)}, u32[]{:S(2)}, u32[]{:S(2)}) collective-permute-start(f32[128,512]{1,0:T(8,128)} %bitcast.209), channel_id=1, source_target_pairs={{0,11},{1,12},{2,13},{3,14},{4,15},{5,0},{6,1},{7,2},{8,3},{9,4},{... | collective-permute-start | bytes 786440 | tf_op jit(solution)/shard_map/ppermute | solution.py:16
  391.3 5.5 %copy-start.13 = (pred[16]{0:T(512)(128)(4,1)S(1)}, pred[16]{0:T(512)(128)(4,1)}, u32[]{:S(2)}) copy-start(pred[16]{0:T(512)(128)(4,1)} %iota_compare_fusion.2) | copy-start | bytes 52
  391.3 5.5 %copy-start.14 = (pred[16]{0:T(512)(128)(4,1)S(1)}, pred[16]{0:T(512)(128)(4,1)}, u32[]{:S(2)}) copy-start(pred[16]{0:T(512)(128)(4,1)} %iota_compare_fusion.3) | copy-start | bytes 52
Sparse Core Ops, SparseCore 0:
  205.5 147.6 all-reduce.4
where the time goes:
time: 417 us; the launch traced here: 411 us
  waiting for transfers between devices  109 us (26%)
  local copies, waits for them, and re-layouts  96 us (23%)
  blocking collectives  69.7 us (17%)
  other arithmetic  50.7 us (12%)
  starting transfers between devices  35.4 us (8%)
  matrix products  34.3 us (8%)
  between operations  15.2 us (4%)
    psum x1, waiting for transfers between devices, shards(): lax.psum((jnp.sum(key_part[:, :, 1:1 + NV], axis=1), jnp.sum(value_part[:...  76.6 us
    psum x1, blocking collectives, shards(): vert_keys, vert_values = lax.psum((picked_keys, picked_values), 'ctx')  69.7 us
    ppermute x20, starting transfers between devices, from_behind(): lax.ppermute(shard, axis, [(i, (i + by) % peers) for i in range(peers)])  35.4 us
    ppermute x20, waiting for transfers between devices, from_behind(): lax.ppermute(shard, axis, [(i, (i + by) % peers) for i in range(peers)])  32.8 us
    unnamed x52, local copies, waits for them, and re-layouts  19 us
    dot_general x4, matrix products, head_pass(): jnp.einsum('jrgd,jkd->jrgk', grad_head, values_cand, preferred_element_ty...  9.6 us
    dot_general x4, matrix products, head_pass(): jnp.einsum('jrgk,jrgd->jkd', weights_low, grad_head, preferred_element_ty...  9.26 us
  transfers between devices with their start and end apart: 21, of which 5 were waited for; matrix products, arithmetic and copies ran while one was open for 17% of the time, Pallas kernels for 0%

commit v1 on v0

v1 whole, which is shorter than its diff:
```python
import functools
import math

import jax
import jax.numpy as jnp
from jax import lax
from jax.experimental import pallas as pl
from jax.experimental.pallas import tpu as pltpu
from jax.sharding import PartitionSpec as P

BLOCK = 64
WDEV = 5
NV = 8
SLASH_COUNT = 3
NEG = -1e30
LIMIT = 48 * 1024 * 1024
MESH = pl.DeviceIdType.MESH


def pick_kernel(per_device, devices, me_ref, slab_ref, vert_ref, ck, cv, pk, src, pick_sem, src_sem):
    me = me_ref[0]
    slab = slab_ref[0]
    heads = vert_ref.shape[0]
    dim = ck.shape[2] // heads
    copies = []
    for which in range(2):
        for kind, ref in enumerate((ck, cv)):
            copy = pltpu.make_async_copy(
                ref.at[slab - which], src.at[which, kind], src_sem.at[which, kind]
            )
            copy.start()
            copies.append(copy)
    pk[...] = jnp.zeros_like(pk)

    def owned_copies(h, v):
        block = vert_ref[h, v]
        region = block // (per_device * devices)
        inner = block % (per_device * devices)
        start = pl.multiple_of((inner % per_device) * BLOCK, BLOCK)
        mine = inner // per_device == me
        made = [
            pltpu.make_async_copy(
                ref.at[region, pl.ds(start, BLOCK), pl.ds(h * dim, dim)],
                pk.at[h * NV + v, kind],
                pick_sem.at[h * NV + v, kind],
            )
            for kind, ref in enumerate((ck, cv))
        ]
        return mine, made

    for h in range(heads):
        for v in range(NV):
            mine, made = owned_copies(h, v)

            @pl.when(mine)
            def _():
                for copy in made:
                    copy.start()

    for copy in copies:
        copy.wait()
    for h in range(heads):
        for v in range(NV):
            mine, made = owned_copies(h, v)

            @pl.when(mine)
            def _():
                for copy in made:
                    copy.wait()


def add_rows(target, target_at, parts, count):
    step = min(count, 64)

    def one(i, carry):
        at = pl.multiple_of(i * step, step)
        total = None
        for ref, start in parts:
            rows = ref[pl.ds(pl.multiple_of(start + at, step), step), :].astype(jnp.float32)
            total = rows if total is None else total + rows
        target[pl.ds(pl.multiple_of(target_at + at, step), step), :] = total.astype(target.dtype)
        return carry

    lax.fori_loop(0, count // step, one, 0)


def exchange_kernel(
    devices,
    back,
    src,
    vert,
    win,
    out,
    got1,
    got2,
    got3,
    sum1,
    sum2,
    win_send,
    win_recv,
    own_sem,
    send,
    recv,
    far_send,
    far_recv,
    gather_send,
    gather_recv,
):
    me = lax.axis_index("ctx")
    rows = vert.shape[0]
    half, quarter = rows // 2, rows // 4
    far = devices // 4
    piece = rows // devices
    c, x, z = me % 2, (me // 2) % 2, me // 4
    core_peer = me + 1 - 2 * c
    x_peer = me + 2 - 4 * x

    barrier = pltpu.get_barrier_semaphore()

    def greet(k, carry):
        pl.semaphore_signal(
            barrier, inc=1, device_id={"ctx": (me + k) % devices}, device_id_type=MESH
        )
        return carry

    lax.fori_loop(1, devices, greet, 0)
    pl.semaphore_wait(barrier, devices - 1)

    def remote(a, b, s, r, peer):
        return pltpu.make_async_remote_copy(
            src_ref=a, dst_ref=b, send_sem=s, recv_sem=r, device_id={"ctx": peer}, device_id_type=MESH
        )

    def at(ref, start, count):
        return ref.at[pl.ds(pl.multiple_of(start, count), count)]

    first = remote(at(vert, (1 - c) * half, half), got1, send.at[0], recv.at[0], core_peer)
    first.start()
    window = []
    for d in range(1, WDEV + 1):
        if back:
            copy = remote(
                src.at[WDEV - d],
                win.at[d - 1],
                win_send.at[d - 1],
                win_recv.at[d - 1],
                (me + devices - d) % devices,
            )
        else:
            copy = remote(
                src.at[(me + d) // devices],
                win.at[WDEV - d],
                win_send.at[d - 1],
                win_recv.at[d - 1],
                (me + d) % devices,
            )
        window.append(copy)
    own = None
    if not back:
        own = pltpu.make_async_copy(src.at[0], win.at[WDEV], own_sem.at[0])
        own.start()
    first.wait()
    for copy in window:
        copy.start()
    add_rows(sum1, 0, [(vert, c * half), (got1, 0)], half)
    second = remote(at(sum1, (1 - x) * quarter, quarter), got2, send.at[1], recv.at[1], x_peer)
    second.start()
    second.wait()
    add_rows(sum2, 0, [(sum1, x * quarter), (got2, 0)], quarter)
    spread = []
    for k in range(1, far):
        peer_z = (z + k) % far
        copy = remote(
            at(sum2, peer_z * piece, piece),
            got3.at[pl.ds((k - 1) * piece, piece)],
            far_send.at[k - 1],
            far_recv.at[k - 1],
            peer_z * 4 + me % 4,
        )
        copy.start()
        spread.append(copy)
    for copy in spread:
        copy.wait()
    base = c * half + x * quarter + z * piece
    add_rows(
        out, base, [(sum2, z * piece)] + [(got3, k * piece) for k in range(far - 1)], piece
    )
    gathered = []
    for k in range(1, far):
        peer_z = (z + k) % far
        copy = remote(
            at(out, base, piece),
            at(out, base, piece),
            gather_send.at[k - 1],
            gather_recv.at[k - 1],
            peer_z * 4 + me % 4,
        )
        copy.start()
        gathered.append(copy)
    for copy in gathered:
        copy.wait()
    third = remote(
        at(out, c * half + x * quarter, quarter),
        at(out, c * half + x * quarter, quarter),
        send.at[2],
        recv.at[2],
        x_peer,
    )
    third.start()
    third.wait()
    fourth = remote(at(out, c * half, half), at(out, c * half, half), send.at[3], recv.at[3], core_peer)
    fourth.start()
    fourth.wait()
    if own is not None:
        own.wait()
    for copy in window:
        copy.wait()


def exchange(src, vert, devices, back):
    rows, dim = vert.shape
    far = devices // 4
    piece = rows // devices
    slots = WDEV if back else WDEV + 1
    dma = pltpu.SemaphoreType.DMA
    return pl.pallas_call(
        functools.partial(exchange_kernel, devices, back),
        out_shape=(
            jax.ShapeDtypeStruct((slots,) + src.shape[1:], jnp.bfloat16),
            jax.ShapeDtypeStruct((rows, dim), jnp.bfloat16),
        ),
        in_specs=[
            pl.BlockSpec(memory_space=pl.ANY),
            pl.BlockSpec(memory_space=pltpu.VMEM),
        ],
        out_specs=(
            pl.BlockSpec(memory_space=pl.ANY),
            pl.BlockSpec(memory_space=pltpu.VMEM),
        ),
        scratch_shapes=[
            pltpu.VMEM((rows // 2, dim), jnp.bfloat16),
            pltpu.VMEM((rows // 4, dim), jnp.bfloat16),
            pltpu.VMEM(((far - 1) * piece, dim), jnp.bfloat16),
            pltpu.VMEM((rows // 2, dim), jnp.bfloat16),
            pltpu.VMEM((rows // 4, dim), jnp.bfloat16),
            dma((WDEV,)),
            dma((WDEV,)),
            dma((1,)),
            dma((4,)),
            dma((4,)),
            dma((far - 1,)),
            dma((far - 1,)),
            dma((far - 1,)),
            dma((far - 1,)),
        ],
        compiler_params=pltpu.CompilerParams(
            collective_id=1 if back else 0, has_side_effects=True, vmem_limit_bytes=LIMIT
        ),
        name="send_back" if back else "send_out",
    )(src, vert)


def attend_kernel(
    per_device,
    first_ref,
    vert_ref,
    off_ref,
    q_ref,
    g_ref,
    f_ref,
    win_ref,
    vb_ref,
    dq_ref,
    near_ref,
    dvert_ref,
    near,
    dvert,
    w_low,
    s_low,
):
    h = pl.program_id(0)
    dim = win_ref.shape[3]
    group = q_ref.shape[1] // dim
    lanes = group * BLOCK
    scaling = 1.0 / math.sqrt(dim)
    near[...] = jnp.zeros_like(near)
    position = lax.broadcasted_iota(jnp.int32, (BLOCK, lanes), 1) % BLOCK
    causal = lax.broadcasted_iota(jnp.int32, (BLOCK, lanes), 0) <= position
    contract_last = (((1,), (1,)), ((), ()))
    contract_first = (((0,), (0,)), ((), ()))
    for j in range(per_device):
        block = first_ref[0] + j

        def stacked(ref):
            return jnp.concatenate(
                [
                    ref[j * BLOCK : (j + 1) * BLOCK, a * dim : (a + 1) * dim]
                    for a in range(group)
                ],
                axis=0,
            )

        q, g, f = stacked(q_ref), stacked(g_ref), stacked(f_ref)
        delta = jnp.sum(
            (g.astype(jnp.float32) * f.astype(jnp.float32)).T, axis=0, keepdims=True
        )
        places, biases = [WDEV * per_device + j], [None]
        for v in range(NV):
            biases.append(jnp.where(vert_ref[h, v] < block, 0.0, NEG))
        for s in range(SLASH_COUNT):
            offset = off_ref[h, s]
            valid = offset > 0
            for v in range(NV):
                valid = valid & (vert_ref[h, v] != block - offset)
            biases.append(jnp.where(valid, 0.0, NEG))
            places.append(WDEV * per_device + j - offset)

        def near_rows(place, kind):
            start = pl.multiple_of((place % per_device) * BLOCK, BLOCK)
            return win_ref[place // per_device, kind, pl.ds(start, BLOCK), :]

        def candidates(kind):
            return jnp.concatenate(
                [near_rows(places[0], kind)]
                + [vb_ref[v, kind] for v in range(NV)]
                + [near_rows(p, kind) for p in places[1:]],
                axis=0,
            )

        keys, values = candidates(0), candidates(1)
        count = len(biases)
        scores = lax.dot_general(keys, q, contract_last, preferred_element_type=jnp.float32)
        masked = []
        for n in range(count):
            part = scores[n * BLOCK : (n + 1) * BLOCK]
            masked.append(
                jnp.where(causal, part, NEG) if n == 0 else part + biases[n]
            )
        top = masked[0]
        for part in masked[1:]:
            top = jnp.maximum(top, part)
        top = jnp.max(top, axis=0, keepdims=True)
        raised = [jnp.exp((part - top) * scaling) for part in masked]
        total = raised[0]
        for part in raised[1:]:
            total = total + part
        inverse = 1.0 / jnp.sum(total, axis=0, keepdims=True)
        weight_grad = lax.dot_general(
            values, g, contract_last, preferred_element_type=jnp.float32
        )
        for n in range(count):
            rows = slice(n * BLOCK, (n + 1) * BLOCK)
            weights = raised[n] * inverse
            w_low[rows, :] = weights.astype(jnp.bfloat16)
            s_low[rows, :] = (weights * (weight_grad[rows] - delta)).astype(jnp.bfloat16)
        score_low = s_low[...]
        dv = jnp.dot(w_low[...], g, preferred_element_type=jnp.float32)
        dk = jnp.dot(score_low, q, preferred_element_type=jnp.float32) * scaling
        dq = lax.dot_general(keys, score_low, contract_first, preferred_element_type=jnp.float32)
        dq = (dq * scaling).T.astype(jnp.bfloat16)
        for a in range(group):
            dq_ref[j * BLOCK : (j + 1) * BLOCK, a * dim : (a + 1) * dim] = dq[
                a * BLOCK : (a + 1) * BLOCK
            ]
        for kind, grads in enumerate((dk, dv)):
            near[places[0], kind] += grads[:BLOCK]
            for s in range(SLASH_COUNT):
                low = (1 + NV + s) * BLOCK
                near[places[1 + s], kind] += grads[low : low + BLOCK]
            for v in range(NV):
                part = grads[(1 + v) * BLOCK : (2 + v) * BLOCK]
                if j == 0:
                    dvert[v, kind] = part
                else:
                    dvert[v, kind] += part
    for p in range((WDEV + 1) * per_device):
        low = (p % per_device) * BLOCK
        near_ref[p // per_device, :, low : low + BLOCK, :] = near[p].astype(jnp.bfloat16)
    dvert_ref[...] = dvert[...].astype(jnp.bfloat16)


def gather_kernel(
    per_device, devices, me_ref, slab_ref, vert_ref, near, back, vb, dk, dv
):
    me = me_ref[0]
    slab = slab_ref[0]
    heads = vert_ref.shape[0]
    dim = vb.shape[3]
    outs = (dk, dv)
    for out in outs:
        out[...] = jnp.zeros_like(out)
    for h in range(heads):
        for v in range(NV):
            block = vert_ref[h, v]
            inner = block % (per_device * devices)

            @pl.when(inner // per_device == me)
            def _():
                region = block // (per_device * devices)
                start = pl.multiple_of((inner % per_device) * BLOCK, BLOCK)
                for kind, out in enumerate(outs):
                    out[region, pl.ds(start, BLOCK), h * dim : (h + 1) * dim] = vb[
                        h * NV + v, kind
                    ]

    here = [
        jnp.where(me + d < devices, 1.0, 0.0).astype(jnp.float32) for d in range(1, WDEV + 1)
    ]
    for kind, out in enumerate(outs):
        current = out[slab].astype(jnp.float32) + near[WDEV, kind].astype(jnp.float32)
        for d in range(1, WDEV + 1):
            current = current + back[d - 1, kind].astype(jnp.float32) * here[d - 1]
        out[slab] = current.astype(jnp.bfloat16)

        @pl.when(me + WDEV >= devices)
        def _():
            prior = out[slab - 1].astype(jnp.float32)
            for d in range(1, WDEV + 1):
                prior = prior + back[d - 1, kind].astype(jnp.float32) * (1.0 - here[d - 1])
            out[slab - 1] = prior.astype(jnp.bfloat16)


def shards(
    queries,
    context_keys,
    context_values,
    forward_output,
    output_cotangent,
    verticals,
    offsets,
    slab_index,
):
    devices = lax.axis_size("ctx")
    me = lax.axis_index("ctx").astype(jnp.int32)
    row_count, columns = queries.shape
    regions, _, features = context_keys.shape
    heads = verticals.shape[0]
    dim = features // heads
    per_device = row_count // BLOCK
    wide = columns // heads
    smem = pl.BlockSpec(memory_space=pltpu.SMEM)
    vmem = pl.BlockSpec(memory_space=pltpu.VMEM)
    hbm = pl.BlockSpec(memory_space=pl.ANY)
    params = pltpu.CompilerParams(vmem_limit_bytes=LIMIT)
    me_arr = me[None]
    low = jnp.bfloat16
    dma = pltpu.SemaphoreType.DMA
    picked, src = pl.pallas_call(
        functools.partial(pick_kernel, per_device, devices),
        out_shape=(
            jax.ShapeDtypeStruct((heads * NV, 2, BLOCK, dim), low),
            jax.ShapeDtypeStruct((2, 2, row_count, features), low),
        ),
        in_specs=[smem, smem, smem, hbm, hbm],
        out_specs=(vmem, vmem),
        scratch_shapes=[dma((heads * NV, 2)), dma((2, 2))],
        compiler_params=params,
        name="pick",
    )(me_arr, slab_index, verticals, context_keys, context_values)
    win, vert = exchange(src, picked.reshape(-1, dim), devices, False)
    first_block = slab_index * (per_device * devices) + me * per_device
    head_rows = pl.BlockSpec((row_count, wide), lambda h, *_: (0, h))
    near_spec = pl.BlockSpec((WDEV + 1, 2, row_count, dim), lambda h, *_: (0, 0, 0, h))
    vert_spec = pl.BlockSpec((NV, 2, BLOCK, dim), lambda h, *_: (h, 0, 0, 0))
    count = 1 + NV + SLASH_COUNT
    lanes = wide // dim * BLOCK
    query_grad, near, vert_grad = pl.pallas_call(
        functools.partial(attend_kernel, per_device),
        out_shape=(
            jax.ShapeDtypeStruct((row_count, columns), low),
            jax.ShapeDtypeStruct((WDEV + 1, 2, row_count, features), low),
            jax.ShapeDtypeStruct((heads * NV, 2, BLOCK, dim), low),
        ),
        grid_spec=pltpu.PrefetchScalarGridSpec(
            num_scalar_prefetch=3,
            grid=(heads,),
            in_specs=[head_rows, head_rows, head_rows, near_spec, vert_spec],
            out_specs=(head_rows, near_spec, vert_spec),
            scratch_shapes=[
                pltpu.VMEM(((WDEV + 1) * per_device, 2, BLOCK, dim), jnp.float32),
                pltpu.VMEM((NV, 2, BLOCK, dim), jnp.float32),
                pltpu.VMEM((count * BLOCK, lanes), low),
                pltpu.VMEM((count * BLOCK, lanes), low),
            ],
        ),
        compiler_params=params,
        name="attend",
    )(
        first_block,
        verticals,
        offsets,
        queries,
        output_cotangent,
        forward_output,
        win,
        vert.reshape(heads * NV, 2, BLOCK, dim),
    )
    back, vert_sum = exchange(near, vert_grad.reshape(-1, dim), devices, True)
    key_grad, value_grad = pl.pallas_call(
        functools.partial(gather_kernel, per_device, devices),
        out_shape=(
            jax.ShapeDtypeStruct((regions, row_count, features), low),
            jax.ShapeDtypeStruct((regions, row_count, features), low),
        ),
        in_specs=[smem, smem, smem, vmem, vmem, vmem],
        out_specs=(vmem, vmem),
        compiler_params=params,
        name="assemble",
    )(
        me_arr,
        slab_index,
        verticals,
        near,
        back,
        vert_sum.reshape(heads * NV, 2, BLOCK, dim),
    )
    return query_grad, key_grad, value_grad


def solution(mesh):
    in_specs = (
        P(("groups", "ctx"), None),
        P("groups", "ctx", None),
        P("groups", "ctx", None),
        P(("groups", "ctx"), None),
        P(("groups", "ctx"), None),
        P("groups", None),
        P("groups", None),
        P("groups"),
    )
    out_specs = (P(("groups", "ctx"), None), P("groups", "ctx", None), P("groups", "ctx", None))
    return jax.shard_map(shards, mesh=mesh, in_specs=in_specs, out_specs=out_specs, check_vma=False)
```

time: 417 us -> 137 us (0.33)
  the two profiles are of different devices: /device:TPU:25 before, /device:TPU:7 now
where the time goes in v1:
time: 137 us
  Pallas kernels  129 us (94%)
  local copies, waits for them, and re-layouts  6.44 us (5%)
    pallas_call x2, Pallas kernels, exchange(): pl.pallas_call(functools.partial(exchange_kernel, devices, back), out_sha...  109 us
    pallas_call x1, Pallas kernels, shards(): pl.pallas_call(functools.partial(attend_kernel, per_device), out_shape=(j...  13.9 us
    unnamed x22, local copies, waits for them, and re-layouts  6.44 us
    pallas_call x1, Pallas kernels, shards(): pl.pallas_call(functools.partial(gather_kernel, per_device, devices), out...  3.74 us
    pallas_call x1, Pallas kernels, shards(): pl.pallas_call(functools.partial(pick_kernel, per_device, devices), out_s...  3.12 us

profile of v1, /device:TPU:7, one launch (start us, length us, event | category | flops | bytes accessed | tf_op | source)
XLA Modules:
  0.0 137.0 jit_solution(7067210370342068262)
XLA Ops:
  1.3 0.0 copy-start.2
  1.3 1.6 %copy-done.2 = bf16[16,128,512]{2,1,0:T(8,128)(2,1)S(1)} copy-done((bf16[16,128,512]{2,1,0:T(8,128)(2,1)S(1)}, bf16[16,128,512]{2,1,0:T(8,128)(2,1)}, u32[]{:S(2)}) %copy-start.2) | copy-done | bytes 2097176
  2.9 0.0 copy-start.3
  2.9 1.6 %copy-done.3 = bf16[16,128,512]{2,1,0:T(8,128)(2,1)S(1)} copy-done((bf16[16,128,512]{2,1,0:T(8,128)(2,1)S(1)}, bf16[16,128,512]{2,1,0:T(8,128)(2,1)}, u32[]{:S(2)}) %copy-start.3) | copy-done | bytes 2097176
  4.5 0.0 copy-start.8
  4.5 0.7 copy-done.8
  5.2 0.0 copy-start.5
  5.2 0.0 copy-start.6
  5.2 0.0 copy-start.7
  5.2 0.0 copy-start.10
  5.2 3.1 %pick.1 = (bf16[32,2,64,128]{3,2,1,0:T(8,128)(2,1)S(1)}, bf16[2,2,128,512]{3,2,1,0:T(8,128)(2,1)S(1)}) custom-call(s32[1]{0:T(128)} %bitcast.1.me_ref, s32[1]{0:T(128)S(6)} %copy.11.slab_ref, s32[4,8]{1,0:T(4,128)S(1)} %copy-done.8, bf16[16,128,512]{2,1,0:T(8,128)(2,1)S(1)} %copy-done.2, bf16[16,128,512]{2,1,0:T(8,128)(2,1)S(1)} %copy-done.3), custom_call_target="tpu_custom_call" | custom-call | tf_op jit(solution)/shard_map/pick/pallas_call | solution.py:448
  8.3 51.9 %send_out.1 = (bf16[6,2,128,512]{3,2,1,0:T(8,128)(2,1)S(1)}, bf16[4096,128]{1,0:T(8,128)(2,1)S(1)}) custom-call(bf16[2,2,128,512]{3,2,1,0:T(8,128)(2,1)S(1)} %get-tuple-element.14.src, bf16[4096,128]{1,0:T(8,128)(2,1)S(1)} %bitcast.6), custom_call_target="tpu_custom_call" | custom-call | tf_op jit(solution)/shard_map/send_out/pallas_call | solution.py:226
  60.2 0.0 copy-start.4
  60.2 1.1 copy-done.4
  61.4 0.0 copy-done.5
  61.4 0.0 copy-done.6
  61.4 0.0 copy-done.7
  61.4 0.0 copy-done.10
  61.4 13.9 %attend.1 = (bf16[128,4096]{1,0:T(8,128)(2,1)}, bf16[6,2,128,512]{3,2,1,0:T(8,128)(2,1)}, bf16[32,2,64,128]{3,2,1,0:T(8,128)(2,1)S(1)}) custom-call(s32[1]{0:T(128)S(6)} %add.7.first_ref, s32[4,8]{1,0:T(4,128)S(1)} %copy-done.8, s32[4,3]{1,0:T(4,128)S(1)} %copy-done.10, bf16[128,4096]{1,0:T(8,128)(2,1)S(1)} %copy-done.5, bf16[128,4096]{1,0:T(8,128)(2,1)S(1)} %copy-done.6, ...), custom_call_target="tpu_custom_call" | custom-call | tf_op jit(solution)/shard_map/attend/pallas_call | solution.py:467
  75.3 0.0 copy-start.9
  75.3 0.0 copy-start
  75.3 1.4 %copy-done = bf16[6,2,128,512]{3,2,1,0:T(8,128)(2,1)S(1)} copy-done((bf16[6,2,128,512]{3,2,1,0:T(8,128)(2,1)S(1)}, bf16[6,2,128,512]{3,2,1,0:T(8,128)(2,1)}, u32[]{:S(2)}) %copy-start) | copy-done | bytes 1572888
  76.7 0.0 copy-start.1
  76.7 56.6 %send_back.1 = (bf16[5,2,128,512]{3,2,1,0:T(8,128)(2,1)S(1)}, bf16[4096,128]{1,0:T(8,128)(2,1)S(1)}) custom-call(bf16[6,2,128,512]{3,2,1,0:T(8,128)(2,1)S(1)} %copy-done, bf16[4096,128]{1,0:T(8,128)(2,1)S(1)} %bitcast.7), custom_call_target="tpu_custom_call" | custom-call | tf_op jit(solution)/shard_map/send_back/pallas_call | solution.py:226
  133.3 0.0 copy-done.9
  133.3 0.0 copy-done.1
  133.3 3.7 %assemble.1 = (bf16[16,128,512]{2,1,0:T(8,128)(2,1)}, bf16[16,128,512]{2,1,0:T(8,128)(2,1)}) custom-call(s32[1]{0:T(128)} %bitcast.1.me_ref, s32[1]{0:T(128)S(6)} %copy.11.slab_ref, s32[4,8]{1,0:T(4,128)S(1)} %copy-done.9, bf16[6,2,128,512]{3,2,1,0:T(8,128)(2,1)S(1)} %copy-done.1, bf16[5,2,128,512]{3,2,1,0:T(8,128)(2,1)S(1)} %get-tuple-element.21.back, ...), custom_call_target="tpu_custom_call" | custom-call | tf_op jit(solution)/shard_map/assemble/pallas_call | solution.py:499
Async XLA Ops:
  1.3 1.6 %copy-start.2 = (bf16[16,128,512]{2,1,0:T(8,128)(2,1)S(1)}, bf16[16,128,512]{2,1,0:T(8,128)(2,1)}, u32[]{:S(2)}) copy-start(bf16[16,128,512]{2,1,0:T(8,128)(2,1)} %ck.1) | copy-start | bytes 6291460
  2.9 1.6 %copy-start.3 = (bf16[16,128,512]{2,1,0:T(8,128)(2,1)S(1)}, bf16[16,128,512]{2,1,0:T(8,128)(2,1)}, u32[]{:S(2)}) copy-start(bf16[16,128,512]{2,1,0:T(8,128)(2,1)} %cv.1) | copy-start | bytes 6291460
  4.5 0.7 copy-start.8
  5.2 56.2 %copy-start.5 = (bf16[128,4096]{1,0:T(8,128)(2,1)S(1)}, bf16[128,4096]{1,0:T(8,128)(2,1)}, u32[]{:S(2)}) copy-start(bf16[128,4096]{1,0:T(8,128)(2,1)} %q_ref.1) | copy-start | bytes 3145732
  5.2 56.2 %copy-start.6 = (bf16[128,4096]{1,0:T(8,128)(2,1)S(1)}, bf16[128,4096]{1,0:T(8,128)(2,1)}, u32[]{:S(2)}) copy-start(bf16[128,4096]{1,0:T(8,128)(2,1)} %g_ref.1) | copy-start | bytes 3145732
  5.2 56.2 %copy-start.7 = (bf16[128,4096]{1,0:T(8,128)(2,1)S(1)}, bf16[128,4096]{1,0:T(8,128)(2,1)}, u32[]{:S(2)}) copy-start(bf16[128,4096]{1,0:T(8,128)(2,1)} %f_ref.1) | copy-start | bytes 3145732
  5.2 56.2 %copy-start.10 = (s32[4,3]{1,0:T(4,128)S(1)}, s32[4,3]{1,0:T(4,128)}, u32[]{:S(2)}) copy-start(s32[4,3]{1,0:T(4,128)} %off_ref.1) | copy-start | bytes 148
  60.2 1.1 copy-start.4
  75.3 58.0 %copy-start.9 = (s32[4,8]{1,0:T(4,128)S(1)}, s32[4,8]{1,0:T(4,128)}, u32[]{:S(2)}) copy-start(s32[4,8]{1,0:T(4,128)} %vert_ref.5) | copy-start | bytes 388
  75.3 1.4 %copy-start = (bf16[6,2,128,512]{3,2,1,0:T(8,128)(2,1)S(1)}, bf16[6,2,128,512]{3,2,1,0:T(8,128)(2,1)}, u32[]{:S(2)}) copy-start(bf16[6,2,128,512]{3,2,1,0:T(8,128)(2,1)} %get-tuple-element.19.src.near) | copy-start | bytes 4718596
  76.7 56.6 %copy-start.1 = (bf16[6,2,128,512]{3,2,1,0:T(8,128)(2,1)S(1)}, bf16[6,2,128,512]{3,2,1,0:T(8,128)(2,1)}, u32[]{:S(2)}) copy-start(bf16[6,2,128,512]{3,2,1,0:T(8,128)(2,1)} %get-tuple-element.19.src.near) | copy-start | bytes 4718596

commit v2 on v1

--- a/solution.py
+++ b/solution.py
@@ -13,6 +13,8 @@
 NV = 8
 SLASH_COUNT = 3
 NEG = -1e30
+STRIDE = 4
+CHUNKS = 4
 LIMIT = 48 * 1024 * 1024
 MESH = pl.DeviceIdType.MESH
 
@@ -87,6 +89,7 @@
 def exchange_kernel(
     devices,
     back,
+    chunks,
     src,
     vert,
     win,
@@ -96,6 +99,8 @@
     got3,
     sum1,
     sum2,
+    joined,
+    from_core,
     win_send,
     win_recv,
     own_sem,
@@ -103,17 +108,14 @@
     recv,
     far_send,
     far_recv,
-    gather_send,
-    gather_recv,
 ):
     me = lax.axis_index("ctx")
-    rows = vert.shape[0]
-    half, quarter = rows // 2, rows // 4
     far = devices // 4
-    piece = rows // devices
     c, x, z = me % 2, (me // 2) % 2, me // 4
     core_peer = me + 1 - 2 * c
     x_peer = me + 2 - 4 * x
+    rows = vert.shape[0] // chunks
+    half, quarter, piece = rows // 2, rows // 4, rows // devices
 
     barrier = pltpu.get_barrier_semaphore()
 
@@ -134,124 +136,166 @@
     def at(ref, start, count):
         return ref.at[pl.ds(pl.multiple_of(start, count), count)]
 
-    first = remote(at(vert, (1 - c) * half, half), got1, send.at[0], recv.at[0], core_peer)
-    first.start()
-    window = []
-    for d in range(1, WDEV + 1):
-        if back:
-            copy = remote(
-                src.at[WDEV - d],
-                win.at[d - 1],
-                win_send.at[d - 1],
-                win_recv.at[d - 1],
-                (me + devices - d) % devices,
-            )
+    def near(k, a, b, peer):
+        return remote(a, b, win_send.at[k], win_recv.at[k], peer)
+
+    def stage(s, k):
+        base = k * rows
+        own_half = base + c * half
+        own_quarter = own_half + x * quarter
+        own_piece = own_quarter + z * piece
+        if s == 0:
+            a, b, peer = at(vert, base + (1 - c) * half, half), at(got1, k * half, half), core_peer
+        elif s == 1:
+            add_rows(sum1, k * half, [(vert, own_half), (got1, k * half)], half)
+            a = at(sum1, k * half + (1 - x) * quarter, quarter)
+            b, peer = at(got2, k * quarter, quarter), x_peer
+        elif s == 2 or s == 3:
+            if s == 2:
+                add_rows(
+                    sum2, k * quarter, [(sum1, k * half + x * quarter), (got2, k * quarter)], quarter
+                )
+            else:
+                add_rows(
+                    out,
+                    own_piece,
+                    [(sum2, k * quarter + z * piece)]
+                    + [(got3, (k * (far - 1) + n) * piece) for n in range(far - 1)],
+                    piece,
+                )
+            made = []
+            for n in range(1, far):
+                peer_z = (z + n) % far
+                if s == 2:
+                    a = at(sum2, k * quarter + peer_z * piece, piece)
+                    b = at(got3, (k * (far - 1) + n - 1) * piece, piece)
+                else:
+                    a = b = at(out, own_piece, piece)
+                made.append(
+                    remote(
+                        a,
+                        b,
+                        far_send.at[s - 2, k, n - 1],
+                        far_recv.at[s - 2, k, n - 1],
+                        peer_z * 4 + me % 4,
+                    )
+                )
+            return made
+        elif s == 4:
+            a = b = at(out, own_quarter, quarter)
+            peer = x_peer
         else:
-            copy = remote(
-                src.at[(me + d) // devices],
-                win.at[WDEV - d],
-                win_send.at[d - 1],
-                win_recv.at[d - 1],
-                (me + d) % devices,
-            )
-        window.append(copy)
-    own = None
-    if not back:
-        own = pltpu.make_async_copy(src.at[0], win.at[WDEV], own_sem.at[0])
-        own.start()
-    first.wait()
-    for copy in window:
-        copy.start()
-    add_rows(sum1, 0, [(vert, c * half), (got1, 0)], half)
-    second = remote(at(sum1, (1 - x) * quarter, quarter), got2, send.at[1], recv.at[1], x_peer)
-    second.start()
-    second.wait()
-    add_rows(sum2, 0, [(sum1, x * quarter), (got2, 0)], quarter)
-    spread = []
-    for k in range(1, far):
-        peer_z = (z + k) % far
-        copy = remote(
-            at(sum2, peer_z * piece, piece),
-            got3.at[pl.ds((k - 1) * piece, piece)],
-            far_send.at[k - 1],
-            far_recv.at[k - 1],
-            peer_z * 4 + me % 4,
+            a = b = at(out, own_half, half)
+            peer = core_peer
+        slot = s if s < 2 else s - 2
+        return [remote(a, b, send.at[slot, k], recv.at[slot, k], peer)]
+
+    flying = {}
+    for k in range(chunks):
+        flying[k] = stage(0, k)
+        for copy in flying[k]:
+            copy.start()
+    pending = []
+    own = []
+    if back:
+        swaps = [
+            near(n, src.at[place], from_core.at[n], core_peer)
+            for n, place in enumerate((4 - 2 * c, 2 - 2 * c))
+        ]
+        for copy in swaps:
+            copy.start()
+        extra = near(
+            2, src.at[4 * c], win.at[2], (me + devices - 5 + 4 * c) % devices
         )
-        copy.start()
-        spread.append(copy)
-    for copy in spread:
+        extra.start()
+        pending.append(extra)
+        for n, d in enumerate((2, 4)):
+            swaps[n].wait()
+
+            def join(i, carry):
+                at_row = pl.ds(pl.multiple_of(i * 16, 16), 16)
+                for kind in range(2):
+                    joined[n, kind, at_row, :] = (
+                        src[WDEV - d, kind, at_row, :].astype(jnp.float32)
+                        + from_core[n, kind, at_row, :].astype(jnp.float32)
+                    ).astype(jnp.bfloat16)
+                return carry
+
+            lax.fori_loop(0, src.shape[2] // 16, join, 0)
+            copy = near(3 + n, joined.at[n], win.at[n], (me + devices - d) % devices)
+            copy.start()
+            pending.append(copy)
+    else:
+        own.append(pltpu.make_async_copy(src.at[0], win.at[WDEV], own_sem.at[0]))
+        own[0].start()
+        for n, d in enumerate((2, 4)):
+            copy = near(n, src.at[(me + d) // devices], win.at[WDEV - d], (me + d) % devices)
+            copy.start()
+            pending.append(copy)
+        reach = 1 + 4 * c
+        extra = near(
+            2, src.at[(me + reach) // devices], win.at[4 - 4 * c], (me + reach) % devices
+        )
+        extra.start()
+    steps = [(s, k) for s in range(1, 7) for k in range(chunks)]
+    for s, k in sorted(steps, key=lambda step: (STRIDE * step[0] + step[1], -step[0])):
+        for copy in flying[k]:
+            copy.wait()
+        if s < 6:
+            flying[k] = stage(s, k)
+            for copy in flying[k]:
+                copy.start()
+    for copy in own:
         copy.wait()
-    base = c * half + x * quarter + z * piece
-    add_rows(
-        out, base, [(sum2, z * piece)] + [(got3, k * piece) for k in range(far - 1)], piece
-    )
-    gathered = []
-    for k in range(1, far):
-        peer_z = (z + k) % far
-        copy = remote(
-            at(out, base, piece),
-            at(out, base, piece),
-            gather_send.at[k - 1],
-            gather_recv.at[k - 1],
-            peer_z * 4 + me % 4,
-        )
-        copy.start()
-        gathered.append(copy)
-    for copy in gathered:
-        copy.wait()
-    third = remote(
-        at(out, c * half + x * quarter, quarter),
-        at(out, c * half + x * quarter, quarter),
-        send.at[2],
-        recv.at[2],
-        x_peer,
-    )
-    third.start()
-    third.wait()
-    fourth = remote(at(out, c * half, half), at(out, c * half, half), send.at[3], recv.at[3], core_peer)
-    fourth.start()
-    fourth.wait()
-    if own is not None:
-        own.wait()
-    for copy in window:
-        copy.wait()
+    if back:
+        for copy in pending:
+            copy.wait()
+    else:
+        swaps = []
+        for n, d in enumerate((2, 4)):
+            pending[n].wait()
+            place = 2 + 2 * c if n == 0 else 2 * c
+            copy = near(3 + n, win.at[WDEV - d], win.at[place], core_peer)
+            copy.start()
+            swaps.append(copy)
+        extra.wait()
+        for copy in swaps:
+            copy.wait()
 
 
 def exchange(src, vert, devices, back):
     rows, dim = vert.shape
     far = devices // 4
-    piece = rows // devices
-    slots = WDEV if back else WDEV + 1
+    chunks = max(1, min(CHUNKS, rows // (devices * 16)))
+    piece = rows // chunks // devices
+    slots = 3 if back else WDEV + 1
+    slot = (2,) + src.shape[1:] if back else (1, 1, 16, src.shape[3])
     dma = pltpu.SemaphoreType.DMA
+    vmem = pl.BlockSpec(memory_space=pltpu.VMEM)
+    low = jnp.bfloat16
     return pl.pallas_call(
-        functools.partial(exchange_kernel, devices, back),
+        functools.partial(exchange_kernel, devices, back, chunks),
         out_shape=(
-            jax.ShapeDtypeStruct((slots,) + src.shape[1:], jnp.bfloat16),
-            jax.ShapeDtypeStruct((rows, dim), jnp.bfloat16),
+            jax.ShapeDtypeStruct((slots,) + src.shape[1:], low),
+            jax.ShapeDtypeStruct((rows, dim), low),
         ),
-        in_specs=[
-            pl.BlockSpec(memory_space=pl.ANY),
-            pl.BlockSpec(memory_space=pltpu.VMEM),
-        ],
-        out_specs=(
-            pl.BlockSpec(memory_space=pl.ANY),
-            pl.BlockSpec(memory_space=pltpu.VMEM),
-        ),
+        in_specs=[vmem, vmem],
+        out_specs=(vmem, vmem),
         scratch_shapes=[
-            pltpu.VMEM((rows // 2, dim), jnp.bfloat16),
-            pltpu.VMEM((rows // 4, dim), jnp.bfloat16),
-            pltpu.VMEM(((far - 1) * piece, dim), jnp.bfloat16),
-            pltpu.VMEM((rows // 2, dim), jnp.bfloat16),
-            pltpu.VMEM((rows // 4, dim), jnp.bfloat16),
-            dma((WDEV,)),
-            dma((WDEV,)),
+            pltpu.VMEM((rows // 2, dim), low),
+            pltpu.VMEM((rows // 4, dim), low),
+            pltpu.VMEM((chunks * (far - 1) * piece, dim), low),
+            pltpu.VMEM((rows // 2, dim), low),
+            pltpu.VMEM((rows // 4, dim), low),
+            pltpu.VMEM(slot, low),
+            pltpu.VMEM(slot, low),
+            dma((5,)),
+            dma((5,)),
             dma((1,)),
-            dma((4,)),
-            dma((4,)),
-            dma((far - 1,)),
-            dma((far - 1,)),
-            dma((far - 1,)),
-            dma((far - 1,)),
+            dma((4, chunks)),
+            dma((4, chunks)),
+            dma((2, chunks, far - 1)),
+            dma((2, chunks, far - 1)),
         ],
         compiler_params=pltpu.CompilerParams(
             collective_id=1 if back else 0, has_side_effects=True, vmem_limit_bytes=LIMIT
@@ -403,20 +447,21 @@
                         h * NV + v, kind
                     ]
 
-    here = [
-        jnp.where(me + d < devices, 1.0, 0.0).astype(jnp.float32) for d in range(1, WDEV + 1)
+    wrapped = [
+        jnp.where(me + reach >= devices, 1.0, 0.0).astype(jnp.float32)
+        for reach in (2, 4, 1 + 4 * (me % 2))
     ]
     for kind, out in enumerate(outs):
         current = out[slab].astype(jnp.float32) + near[WDEV, kind].astype(jnp.float32)
-        for d in range(1, WDEV + 1):
-            current = current + back[d - 1, kind].astype(jnp.float32) * here[d - 1]
+        for n in range(3):
+            current = current + back[n, kind].astype(jnp.float32) * (1.0 - wrapped[n])
         out[slab] = current.astype(jnp.bfloat16)
 
         @pl.when(me + WDEV >= devices)
         def _():
             prior = out[slab - 1].astype(jnp.float32)
-            for d in range(1, WDEV + 1):
-                prior = prior + back[d - 1, kind].astype(jnp.float32) * (1.0 - here[d - 1])
+            for n in range(3):
+                prior = prior + back[n, kind].astype(jnp.float32) * wrapped[n]
             out[slab - 1] = prior.astype(jnp.bfloat16)
 
 
@@ -440,7 +485,7 @@
     wide = columns // heads
     smem = pl.BlockSpec(memory_space=pltpu.SMEM)
     vmem = pl.BlockSpec(memory_space=pltpu.VMEM)
-    hbm = pl.BlockSpec(memory_space=pl.ANY)
+    hbm = pl.BlockSpec(memory_space=pltpu.HBM)
     params = pltpu.CompilerParams(vmem_limit_bytes=LIMIT)
     me_arr = me[None]
     low = jnp.bfloat16

time: 137 us -> 109 us (0.80)
  the two profiles are of different devices: /device:TPU:7 before, /device:TPU:3 now
where the time goes in v2:
time: 109 us; the launch traced here: 108 us
  Pallas kernels  101 us (93%)
  local copies, waits for them, and re-layouts  6.44 us (6%)
  between operations  1.36 us (1%)
    pallas_call x2, Pallas kernels, exchange(): pl.pallas_call(functools.partial(exchange_kernel, devices, back, chunks),...  80 us
    pallas_call x1, Pallas kernels, shards(): pl.pallas_call(functools.partial(attend_kernel, per_device), out_shape=(j...  13.9 us
    unnamed x22, local copies, waits for them, and re-layouts  6.44 us
    pallas_call x1, Pallas kernels, shards(): pl.pallas_call(functools.partial(gather_kernel, per_device, devices), out...  3.66 us
    pallas_call x1, Pallas kernels, shards(): pl.pallas_call(functools.partial(pick_kernel, per_device, devices), out_s...  3.13 us

profile of v2, /device:TPU:3, one launch (start us, length us, event | category | flops | bytes accessed | tf_op | source)
XLA Modules:
  0.0 108.5 jit_solution(7823904967910803675)
XLA Ops:
  1.3 0.0 copy-start.2
  1.3 1.6 %copy-done.2 = bf16[16,128,512]{2,1,0:T(8,128)(2,1)S(1)} copy-done((bf16[16,128,512]{2,1,0:T(8,128)(2,1)S(1)}, bf16[16,128,512]{2,1,0:T(8,128)(2,1)}, u32[]{:S(2)}) %copy-start.2) | copy-done | bytes 2097176
  2.9 0.0 copy-start.3
  2.9 1.6 %copy-done.3 = bf16[16,128,512]{2,1,0:T(8,128)(2,1)S(1)} copy-done((bf16[16,128,512]{2,1,0:T(8,128)(2,1)S(1)}, bf16[16,128,512]{2,1,0:T(8,128)(2,1)}, u32[]{:S(2)}) %copy-start.3) | copy-done | bytes 2097176
  4.5 0.0 copy-start.8
  4.5 0.7 copy-done.8
  5.2 0.0 copy-start.5
  5.2 0.0 copy-start.6
  5.2 0.0 copy-start.7
  5.2 0.0 copy-start.10
  5.2 3.1 %pick.1 = (bf16[32,2,64,128]{3,2,1,0:T(8,128)(2,1)S(1)}, bf16[2,2,128,512]{3,2,1,0:T(8,128)(2,1)S(1)}) custom-call(s32[1]{0:T(128)} %bitcast.1.me_ref, s32[1]{0:T(128)S(6)} %copy.11.slab_ref, s32[4,8]{1,0:T(4,128)S(1)} %copy-done.8, bf16[16,128,512]{2,1,0:T(8,128)(2,1)S(1)} %copy-done.2, bf16[16,128,512]{2,1,0:T(8,128)(2,1)S(1)} %copy-done.3), custom_call_target="tpu_custom_call" | custom-call | tf_op jit(solution)/shard_map/pick/pallas_call | solution.py:493
  8.3 40.3 %send_out.1 = (bf16[6,2,128,512]{3,2,1,0:T(8,128)(2,1)S(1)}, bf16[4096,128]{1,0:T(8,128)(2,1)S(1)}) custom-call(bf16[2,2,128,512]{3,2,1,0:T(8,128)(2,1)S(1)} %get-tuple-element.14.src, bf16[4096,128]{1,0:T(8,128)(2,1)S(1)} %bitcast.6), custom_call_target="tpu_custom_call" | custom-call | tf_op jit(solution)/shard_map/send_out/pallas_call | solution.py:276
  48.6 0.0 copy-start.4
  48.6 1.1 %copy-done.4 = bf16[6,2,128,512]{3,2,1,0:T(8,128)(2,1)} copy-done((bf16[6,2,128,512]{3,2,1,0:T(8,128)(2,1)}, bf16[6,2,128,512]{3,2,1,0:T(8,128)(2,1)S(1)}, u32[]{:S(2)}) %copy-start.4) | copy-done | bytes 1572888
  49.7 0.0 copy-done.5
  49.7 0.0 copy-done.6
  49.7 0.0 copy-done.7
  49.7 0.0 copy-done.10
  49.7 13.9 %attend.1 = (bf16[128,4096]{1,0:T(8,128)(2,1)}, bf16[6,2,128,512]{3,2,1,0:T(8,128)(2,1)}, bf16[32,2,64,128]{3,2,1,0:T(8,128)(2,1)S(1)}) custom-call(s32[1]{0:T(128)S(6)} %add.7.first_ref, s32[4,8]{1,0:T(4,128)S(1)} %copy-done.8, s32[4,3]{1,0:T(4,128)S(1)} %copy-done.10, bf16[128,4096]{1,0:T(8,128)(2,1)S(1)} %copy-done.5, bf16[128,4096]{1,0:T(8,128)(2,1)S(1)} %copy-done.6, ...), custom_call_target="tpu_custom_call" | custom-call | tf_op jit(solution)/shard_map/attend/pallas_call | solution.py:512
  63.6 0.0 copy-start.9
  63.6 0.0 copy-start
  63.6 1.4 %copy-done = bf16[6,2,128,512]{3,2,1,0:T(8,128)(2,1)S(1)} copy-done((bf16[6,2,128,512]{3,2,1,0:T(8,128)(2,1)S(1)}, bf16[6,2,128,512]{3,2,1,0:T(8,128)(2,1)}, u32[]{:S(2)}) %copy-start) | copy-done | bytes 1572888
  65.0 0.0 copy-start.1
  65.0 39.8 %send_back.1 = (bf16[3,2,128,512]{3,2,1,0:T(8,128)(2,1)S(1)}, bf16[4096,128]{1,0:T(8,128)(2,1)S(1)}) custom-call(bf16[6,2,128,512]{3,2,1,0:T(8,128)(2,1)S(1)} %copy-done, bf16[4096,128]{1,0:T(8,128)(2,1)S(1)} %bitcast.7), custom_call_target="tpu_custom_call" | custom-call | tf_op jit(solution)/shard_map/send_back/pallas_call | solution.py:276
  104.8 0.0 copy-done.9
  104.8 0.0 copy-done.1
  104.8 3.7 %assemble.1 = (bf16[16,128,512]{2,1,0:T(8,128)(2,1)}, bf16[16,128,512]{2,1,0:T(8,128)(2,1)}) custom-call(s32[1]{0:T(128)} %bitcast.1.me_ref, s32[1]{0:T(128)S(6)} %copy.11.slab_ref, s32[4,8]{1,0:T(4,128)S(1)} %copy-done.9, bf16[6,2,128,512]{3,2,1,0:T(8,128)(2,1)S(1)} %copy-done.1, bf16[3,2,128,512]{3,2,1,0:T(8,128)(2,1)S(1)} %get-tuple-element.21.back, ...), custom_call_target="tpu_custom_call" | custom-call | tf_op jit(solution)/shard_map/assemble/pallas_call | solution.py:544
Async XLA Ops:
  1.3 1.6 %copy-start.2 = (bf16[16,128,512]{2,1,0:T(8,128)(2,1)S(1)}, bf16[16,128,512]{2,1,0:T(8,128)(2,1)}, u32[]{:S(2)}) copy-start(bf16[16,128,512]{2,1,0:T(8,128)(2,1)} %ck.1) | copy-start | bytes 6291460
  2.9 1.6 %copy-start.3 = (bf16[16,128,512]{2,1,0:T(8,128)(2,1)S(1)}, bf16[16,128,512]{2,1,0:T(8,128)(2,1)}, u32[]{:S(2)}) copy-start(bf16[16,128,512]{2,1,0:T(8,128)(2,1)} %cv.1) | copy-start | bytes 6291460
  4.5 0.7 copy-start.8
  5.2 44.6 %copy-start.5 = (bf16[128,4096]{1,0:T(8,128)(2,1)S(1)}, bf16[128,4096]{1,0:T(8,128)(2,1)}, u32[]{:S(2)}) copy-start(bf16[128,4096]{1,0:T(8,128)(2,1)} %q_ref.1) | copy-start | bytes 3145732
  5.2 44.6 %copy-start.6 = (bf16[128,4096]{1,0:T(8,128)(2,1)S(1)}, bf16[128,4096]{1,0:T(8,128)(2,1)}, u32[]{:S(2)}) copy-start(bf16[128,4096]{1,0:T(8,128)(2,1)} %g_ref.1) | copy-start | bytes 3145732
  5.2 44.6 %copy-start.7 = (bf16[128,4096]{1,0:T(8,128)(2,1)S(1)}, bf16[128,4096]{1,0:T(8,128)(2,1)}, u32[]{:S(2)}) copy-start(bf16[128,4096]{1,0:T(8,128)(2,1)} %f_ref.1) | copy-start | bytes 3145732
  5.2 44.6 %copy-start.10 = (s32[4,3]{1,0:T(4,128)S(1)}, s32[4,3]{1,0:T(4,128)}, u32[]{:S(2)}) copy-start(s32[4,3]{1,0:T(4,128)} %off_ref.1) | copy-start | bytes 148
  48.6 1.1 %copy-start.4 = (bf16[6,2,128,512]{3,2,1,0:T(8,128)(2,1)}, bf16[6,2,128,512]{3,2,1,0:T(8,128)(2,1)S(1)}, u32[]{:S(2)}) copy-start(bf16[6,2,128,512]{3,2,1,0:T(8,128)(2,1)S(1)} %get-tuple-element.16.win_ref) | copy-start | bytes 4718596
  63.6 41.2 %copy-start.9 = (s32[4,8]{1,0:T(4,128)S(1)}, s32[4,8]{1,0:T(4,128)}, u32[]{:S(2)}) copy-start(s32[4,8]{1,0:T(4,128)} %vert_ref.5) | copy-start | bytes 388
  63.6 1.4 %copy-start = (bf16[6,2,128,512]{3,2,1,0:T(8,128)(2,1)S(1)}, bf16[6,2,128,512]{3,2,1,0:T(8,128)(2,1)}, u32[]{:S(2)}) copy-start(bf16[6,2,128,512]{3,2,1,0:T(8,128)(2,1)} %get-tuple-element.19.src.near) | copy-start | bytes 4718596
  65.0 39.8 %copy-start.1 = (bf16[6,2,128,512]{3,2,1,0:T(8,128)(2,1)S(1)}, bf16[6,2,128,512]{3,2,1,0:T(8,128)(2,1)}, u32[]{:S(2)}) copy-start(bf16[6,2,128,512]{3,2,1,0:T(8,128)(2,1)} %get-tuple-element.19.src.near) | copy-start | bytes 4718596

commit v3 on v2

--- a/solution.py
+++ b/solution.py
@@ -13,7 +13,6 @@
 NV = 8
 SLASH_COUNT = 3
 NEG = -1e30
-STRIDE = 4
 CHUNKS = 4
 LIMIT = 48 * 1024 * 1024
 MESH = pl.DeviceIdType.MESH
@@ -195,8 +194,20 @@
         flying[k] = stage(0, k)
         for copy in flying[k]:
             copy.start()
-    pending = []
-    own = []
+    def joined_rows(n, parts):
+        def join(i, carry):
+            at_row = pl.ds(pl.multiple_of(i * 16, 16), 16)
+            for kind in range(2):
+                total = None
+                for ref, place, weight in parts:
+                    term = ref[place, kind, at_row, :].astype(jnp.float32)
+                    term = term if weight is None else term * weight
+                    total = term if total is None else total + term
+                joined[n, kind, at_row, :] = total.astype(jnp.bfloat16)
+            return carry
+
+        lax.fori_loop(0, src.shape[2] // 16, join, 0)
+
     if back:
         swaps = [
             near(n, src.at[place], from_core.at[n], core_peer)
@@ -204,63 +215,77 @@
         ]
         for copy in swaps:
             copy.start()
-        extra = near(
-            2, src.at[4 * c], win.at[2], (me + devices - 5 + 4 * c) % devices
-        )
+        extra = near(2, src.at[4 * c], win.at[2], (me + devices - 5 + 4 * c) % devices)
         extra.start()
-        pending.append(extra)
-        for n, d in enumerate((2, 4)):
-            swaps[n].wait()
-
-            def join(i, carry):
-                at_row = pl.ds(pl.multiple_of(i * 16, 16), 16)
-                for kind in range(2):
-                    joined[n, kind, at_row, :] = (
-                        src[WDEV - d, kind, at_row, :].astype(jnp.float32)
-                        + from_core[n, kind, at_row, :].astype(jnp.float32)
-                    ).astype(jnp.bfloat16)
-                return carry
-
-            lax.fori_loop(0, src.shape[2] // 16, join, 0)
-            copy = near(3 + n, joined.at[n], win.at[n], (me + devices - d) % devices)
-            copy.start()
-            pending.append(copy)
+        across = near(3, joined.at[0], win.at[0], x_peer)
+        along = near(4, joined.at[1], win.at[1], (me + devices - 4) % devices)
+        swaps[0].wait()
+        joined_rows(0, [(src, WDEV - 2, None), (from_core, 0, None)])
+        swaps[1].wait()
     else:
-        own.append(pltpu.make_async_copy(src.at[0], win.at[WDEV], own_sem.at[0]))
-        own[0].start()
-        for n, d in enumerate((2, 4)):
-            copy = near(n, src.at[(me + d) // devices], win.at[WDEV - d], (me + d) % devices)
-            copy.start()
-            pending.append(copy)
+        own = pltpu.make_async_copy(src.at[0], win.at[WDEV], own_sem.at[0])
+        own.start()
+        along = near(0, src.at[(me + 4) // devices], win.at[WDEV - 4], (me + 4) % devices)
+        along.start()
+        across = near(1, src.at[0], win.at[WDEV - 2], x_peer)
+        passed = near(1, win.at[WDEV - 4], win.at[WDEV - 2], x_peer)
         reach = 1 + 4 * c
-        extra = near(
-            2, src.at[(me + reach) // devices], win.at[4 - 4 * c], (me + reach) % devices
-        )
-        extra.start()
-    steps = [(s, k) for s in range(1, 7) for k in range(chunks)]
-    for s, k in sorted(steps, key=lambda step: (STRIDE * step[0] + step[1], -step[0])):
-        for copy in flying[k]:
-            copy.wait()
-        if s < 6:
-            flying[k] = stage(s, k)
+        extra = near(2, src.at[(me + reach) // devices], win.at[4 - 4 * c], (me + reach) % devices)
+        handed = near(2, win.at[WDEV - 4], win.at[0], (me + 1) % devices)
+        late = c * (1 - x)
+
+        @pl.when(x == 0)
+        def _():
+            across.start()
+
+        @pl.when(late == 0)
+        def _():
+            extra.start()
+
+        swap_far = near(4, win.at[WDEV - 4], win.at[2 * c], core_peer)
+        swap_next = near(3, win.at[WDEV - 2], win.at[2 + 2 * c], core_peer)
+
+    def between(s):
+        if back:
+            if s == 1:
+                across.start()
+            elif s == 3:
+                across.wait()
+                merge = jnp.where(x == 1, 1.0, 0.0).astype(jnp.float32)
+                joined_rows(1, [(src, WDEV - 4, None), (from_core, 1, None), (win, 0, merge)])
+                along.start()
+            elif s == 6:
+                along.wait()
+                extra.wait()
+        elif s == 2:
+            along.wait()
+            swap_far.start()
+
+            @pl.when(x == 1)
+            def _():
+                passed.start()
+
+            @pl.when(late == 1)
+            def _():
+                handed.start()
+        elif s == 4:
+            across.wait()
+            swap_next.start()
+        elif s == 6:
+            extra.wait()
+            swap_far.wait()
+            swap_next.wait()
+            own.wait()
+
+    for s in range(1, 7):
+        for k in range(chunks):
             for copy in flying[k]:
-                copy.start()
-    for copy in own:
-        copy.wait()
-    if back:
-        for copy in pending:
-            copy.wait()
-    else:
-        swaps = []
-        for n, d in enumerate((2, 4)):
-            pending[n].wait()
-            place = 2 + 2 * c if n == 0 else 2 * c
-            copy = near(3 + n, win.at[WDEV - d], win.at[place], core_peer)
-            copy.start()
-            swaps.append(copy)
-        extra.wait()
-        for copy in swaps:
-            copy.wait()
+                copy.wait()
+            if s < 6:
+                flying[k] = stage(s, k)
+                for copy in flying[k]:
+                    copy.start()
+        between(s)
 
 
 def exchange(src, vert, devices, back):
@@ -323,7 +348,8 @@
     s_low,
 ):
     h = pl.program_id(0)
-    dim = win_ref.shape[3]
+    dim = vb_ref.shape[3]
+    columns = pl.ds(pl.multiple_of(h * dim, dim), dim)
     group = q_ref.shape[1] // dim
     lanes = group * BLOCK
     scaling = 1.0 / math.sqrt(dim)
@@ -361,7 +387,7 @@
 
         def near_rows(place, kind):
             start = pl.multiple_of((place % per_device) * BLOCK, BLOCK)
-            return win_ref[place // per_device, kind, pl.ds(start, BLOCK), :]
+            return win_ref[place // per_device, kind, pl.ds(start, BLOCK), columns]
 
         def candidates(kind):
             return jnp.concatenate(
@@ -419,7 +445,7 @@
                     dvert[v, kind] += part
     for p in range((WDEV + 1) * per_device):
         low = (p % per_device) * BLOCK
-        near_ref[p // per_device, :, low : low + BLOCK, :] = near[p].astype(jnp.bfloat16)
+        near_ref[p // per_device, :, low : low + BLOCK, columns] = near[p].astype(jnp.bfloat16)
     dvert_ref[...] = dvert[...].astype(jnp.bfloat16)
 
 
@@ -447,20 +473,23 @@
                         h * NV + v, kind
                     ]
 
-    wrapped = [
-        jnp.where(me + reach >= devices, 1.0, 0.0).astype(jnp.float32)
-        for reach in (2, 4, 1 + 4 * (me % 2))
-    ]
+    def flag(yes):
+        return jnp.where(yes, 1.0, 0.0).astype(jnp.float32)
+
+    far_wraps = me + 4 >= devices
+    extra_wraps = me + 1 + 4 * (me % 2) >= devices
+    here = [flag((me // 2) % 2 == 0), flag(jnp.logical_not(far_wraps)), flag(jnp.logical_not(extra_wraps))]
+    wrapped = [None, flag(far_wraps), flag(extra_wraps)]
     for kind, out in enumerate(outs):
         current = out[slab].astype(jnp.float32) + near[WDEV, kind].astype(jnp.float32)
         for n in range(3):
-            current = current + back[n, kind].astype(jnp.float32) * (1.0 - wrapped[n])
+            current = current + back[n, kind].astype(jnp.float32) * here[n]
         out[slab] = current.astype(jnp.bfloat16)
 
         @pl.when(me + WDEV >= devices)
         def _():
             prior = out[slab - 1].astype(jnp.float32)
-            for n in range(3):
+            for n in range(1, 3):
                 prior = prior + back[n, kind].astype(jnp.float32) * wrapped[n]
             out[slab - 1] = prior.astype(jnp.bfloat16)
 
@@ -499,13 +528,12 @@
         in_specs=[smem, smem, smem, hbm, hbm],
         out_specs=(vmem, vmem),
         scratch_shapes=[dma((heads * NV, 2)), dma((2, 2))],
-        compiler_params=params,
+        compiler_params=pltpu.CompilerParams(vmem_limit_bytes=52 * 1024 * 1024),
         name="pick",
     )(me_arr, slab_index, verticals, context_keys, context_values)
     win, vert = exchange(src, picked.reshape(-1, dim), devices, False)
     first_block = slab_index * (per_device * devices) + me * per_device
     head_rows = pl.BlockSpec((row_count, wide), lambda h, *_: (0, h))
-    near_spec = pl.BlockSpec((WDEV + 1, 2, row_count, dim), lambda h, *_: (0, 0, 0, h))
     vert_spec = pl.BlockSpec((NV, 2, BLOCK, dim), lambda h, *_: (h, 0, 0, 0))
     count = 1 + NV + SLASH_COUNT
     lanes = wide // dim * BLOCK
@@ -519,8 +547,8 @@
         grid_spec=pltpu.PrefetchScalarGridSpec(
             num_scalar_prefetch=3,
             grid=(heads,),
-            in_specs=[head_rows, head_rows, head_rows, near_spec, vert_spec],
-            out_specs=(head_rows, near_spec, vert_spec),
+            in_specs=[head_rows, head_rows, head_rows, vmem, vert_spec],
+            out_specs=(head_rows, vmem, vert_spec),
             scratch_shapes=[
                 pltpu.VMEM(((WDEV + 1) * per_device, 2, BLOCK, dim), jnp.float32),
                 pltpu.VMEM((NV, 2, BLOCK, dim), jnp.float32),
@@ -528,7 +556,7 @@
                 pltpu.VMEM((count * BLOCK, lanes), low),
             ],
         ),
-        compiler_params=params,
+        compiler_params=pltpu.CompilerParams(vmem_limit_bytes=32 * 1024 * 1024),
         name="attend",
     )(
         first_block,

time: 109 us -> 90.1 us (0.83)
  the two profiles are of different devices: /device:TPU:3 before, /device:TPU:25 now
where the time goes in v3:
time: 90.1 us; the launch traced here: 89.9 us
  Pallas kernels  87.9 us (98%)
  between operations  1.36 us (2%)
    pallas_call x2, Pallas kernels, exchange(): pl.pallas_call(functools.partial(exchange_kernel, devices, back, chunks),...  68.3 us
    pallas_call x1, Pallas kernels, shards(): pl.pallas_call(functools.partial(attend_kernel, per_device), out_shape=(j...  12.9 us
    pallas_call x1, Pallas kernels, shards(): pl.pallas_call(functools.partial(gather_kernel, per_device, devices), out...  3.77 us
    pallas_call x1, Pallas kernels, shards(): pl.pallas_call(functools.partial(pick_kernel, per_device, devices), out_s...  2.84 us

profile of v3, /device:TPU:25, one launch (start us, length us, event | category | flops | bytes accessed | tf_op | source)
XLA Modules:
  0.0 89.9 jit_solution(3848132070848574181)
XLA Ops:
  1.3 0.0 copy-start.3
  1.3 0.7 copy-done.3
  2.0 0.0 copy-start
  2.0 0.0 copy-start.1
  2.0 0.0 copy-start.2
  2.0 0.0 copy-start.5
  2.0 2.8 %pick.1 = (bf16[32,2,64,128]{3,2,1,0:T(8,128)(2,1)S(1)}, bf16[2,2,128,512]{3,2,1,0:T(8,128)(2,1)S(1)}) custom-call(s32[1]{0:T(128)} %bitcast.1.me_ref, s32[1]{0:T(128)S(6)} %copy.11.slab_ref, s32[4,8]{1,0:T(4,128)S(1)} %copy-done.3, bf16[16,128,512]{2,1,0:T(8,128)(2,1)} %ck.1, bf16[16,128,512]{2,1,0:T(8,128)(2,1)} %cv.1), custom_call_target="tpu_custom_call" | custom-call | tf_op jit(solution)/shard_map/pick/pallas_call | solution.py:522
  4.8 34.0 %send_out.1 = (bf16[6,2,128,512]{3,2,1,0:T(8,128)(2,1)S(1)}, bf16[4096,128]{1,0:T(8,128)(2,1)S(1)}) custom-call(bf16[2,2,128,512]{3,2,1,0:T(8,128)(2,1)S(1)} %get-tuple-element.14.src, bf16[4096,128]{1,0:T(8,128)(2,1)S(1)} %bitcast.6), custom_call_target="tpu_custom_call" | custom-call | tf_op jit(solution)/shard_map/send_out/pallas_call | solution.py:301
  38.9 0.0 copy-done
  38.9 0.0 copy-done.1
  38.9 0.0 copy-done.2
  38.9 0.0 copy-done.5
  38.9 12.9 %attend.1 = (bf16[128,4096]{1,0:T(8,128)(2,1)}, bf16[6,2,128,512]{3,2,1,0:T(8,128)(2,1)S(1)}, bf16[32,2,64,128]{3,2,1,0:T(8,128)(2,1)S(1)}) custom-call(s32[1]{0:T(128)S(6)} %add.7.first_ref, s32[4,8]{1,0:T(4,128)S(1)} %copy-done.3, s32[4,3]{1,0:T(4,128)S(1)} %copy-done.5, bf16[128,4096]{1,0:T(8,128)(2,1)S(1)} %copy-done, bf16[128,4096]{1,0:T(8,128)(2,1)S(1)} %copy-done.1, ...), custom_call_target="tpu_custom_call" | custom-call | tf_op jit(solution)/shard_map/attend/pallas_call | solution.py:540
  51.8 0.0 copy-start.4
  51.8 34.3 %send_back.1 = (bf16[3,2,128,512]{3,2,1,0:T(8,128)(2,1)S(1)}, bf16[4096,128]{1,0:T(8,128)(2,1)S(1)}) custom-call(bf16[6,2,128,512]{3,2,1,0:T(8,128)(2,1)S(1)} %get-tuple-element.19.src.near, bf16[4096,128]{1,0:T(8,128)(2,1)S(1)} %bitcast.7), custom_call_target="tpu_custom_call" | custom-call | tf_op jit(solution)/shard_map/send_back/pallas_call | solution.py:301
  86.2 0.0 copy-done.4
  86.2 3.8 %assemble.1 = (bf16[16,128,512]{2,1,0:T(8,128)(2,1)}, bf16[16,128,512]{2,1,0:T(8,128)(2,1)}) custom-call(s32[1]{0:T(128)} %bitcast.1.me_ref, s32[1]{0:T(128)S(6)} %copy.11.slab_ref, s32[4,8]{1,0:T(4,128)S(1)} %copy-done.4, bf16[6,2,128,512]{3,2,1,0:T(8,128)(2,1)S(1)} %get-tuple-element.19.src.near, bf16[3,2,128,512]{3,2,1,0:T(8,128)(2,1)S(1)} %get-tuple-element.21.back, ...), custom_call_target="tpu_custom_call" | custom-call | tf_op jit(solution)/shard_map/assemble/pallas_call | solution.py:572
Async XLA Ops:
  1.3 0.7 copy-start.3
  2.0 36.9 %copy-start = (bf16[128,4096]{1,0:T(8,128)(2,1)S(1)}, bf16[128,4096]{1,0:T(8,128)(2,1)}, u32[]{:S(2)}) copy-start(bf16[128,4096]{1,0:T(8,128)(2,1)} %q_ref.1) | copy-start | bytes 3145732
  2.0 36.9 %copy-start.1 = (bf16[128,4096]{1,0:T(8,128)(2,1)S(1)}, bf16[128,4096]{1,0:T(8,128)(2,1)}, u32[]{:S(2)}) copy-start(bf16[128,4096]{1,0:T(8,128)(2,1)} %g_ref.1) | copy-start | bytes 3145732
  2.0 36.9 %copy-start.2 = (bf16[128,4096]{1,0:T(8,128)(2,1)S(1)}, bf16[128,4096]{1,0:T(8,128)(2,1)}, u32[]{:S(2)}) copy-start(bf16[128,4096]{1,0:T(8,128)(2,1)} %f_ref.1) | copy-start | bytes 3145732
  2.0 36.9 %copy-start.5 = (s32[4,3]{1,0:T(4,128)S(1)}, s32[4,3]{1,0:T(4,128)}, u32[]{:S(2)}) copy-start(s32[4,3]{1,0:T(4,128)} %off_ref.1) | copy-start | bytes 148
  51.8 34.3 %copy-start.4 = (s32[4,8]{1,0:T(4,128)S(1)}, s32[4,8]{1,0:T(4,128)}, u32[]{:S(2)}) copy-start(s32[4,8]{1,0:T(4,128)} %vert_ref.5) | copy-start | bytes 388

commit v4 on v3

--- a/solution.py
+++ b/solution.py
@@ -457,6 +457,8 @@
     heads = vert_ref.shape[0]
     dim = vb.shape[3]
     outs = (dk, dv)
+    step = dk.shape[0]
+    g = pl.program_id(0)
     for out in outs:
         out[...] = jnp.zeros_like(out)
     for h in range(heads):
@@ -464,12 +466,13 @@
             block = vert_ref[h, v]
             inner = block % (per_device * devices)
 
-            @pl.when(inner // per_device == me)
+            region = block // (per_device * devices)
+
+            @pl.when((inner // per_device == me) & (region // step == g))
             def _():
-                region = block // (per_device * devices)
                 start = pl.multiple_of((inner % per_device) * BLOCK, BLOCK)
                 for kind, out in enumerate(outs):
-                    out[region, pl.ds(start, BLOCK), h * dim : (h + 1) * dim] = vb[
+                    out[region % step, pl.ds(start, BLOCK), h * dim : (h + 1) * dim] = vb[
                         h * NV + v, kind
                     ]
 
@@ -481,17 +484,22 @@
     here = [flag((me // 2) % 2 == 0), flag(jnp.logical_not(far_wraps)), flag(jnp.logical_not(extra_wraps))]
     wrapped = [None, flag(far_wraps), flag(extra_wraps)]
     for kind, out in enumerate(outs):
-        current = out[slab].astype(jnp.float32) + near[WDEV, kind].astype(jnp.float32)
-        for n in range(3):
-            current = current + back[n, kind].astype(jnp.float32) * here[n]
-        out[slab] = current.astype(jnp.bfloat16)
-
-        @pl.when(me + WDEV >= devices)
+
+        @pl.when(slab // step == g)
         def _():
-            prior = out[slab - 1].astype(jnp.float32)
+            place = slab % step
+            current = out[place].astype(jnp.float32) + near[WDEV, kind].astype(jnp.float32)
+            for n in range(3):
+                current = current + back[n, kind].astype(jnp.float32) * here[n]
+            out[place] = current.astype(jnp.bfloat16)
+
+        @pl.when((me + WDEV >= devices) & ((slab - 1) // step == g))
+        def _():
+            place = (slab - 1) % step
+            prior = out[place].astype(jnp.float32)
             for n in range(1, 3):
                 prior = prior + back[n, kind].astype(jnp.float32) * wrapped[n]
-            out[slab - 1] = prior.astype(jnp.bfloat16)
+            out[place] = prior.astype(jnp.bfloat16)
 
 
 def shards(
@@ -575,8 +583,12 @@
             jax.ShapeDtypeStruct((regions, row_count, features), low),
             jax.ShapeDtypeStruct((regions, row_count, features), low),
         ),
+        grid=(4,),
         in_specs=[smem, smem, smem, vmem, vmem, vmem],
-        out_specs=(vmem, vmem),
+        out_specs=(
+            pl.BlockSpec((regions // 4, row_count, features), lambda g: (g, 0, 0)),
+            pl.BlockSpec((regions // 4, row_count, features), lambda g: (g, 0, 0)),
+        ),
         compiler_params=params,
         name="assemble",
     )(

time: 90.1 us -> 91.9 us (1.020)
  Pallas kernels: 87.9 us -> 89.7 us
    pallas_call x1, Pallas kernels: 3.77 us -> 5.58 us  [shards(): pl.pallas_call(functools.partial(gather_kernel, per_device, devices), out...]
where the time goes in v4:
time: 91.9 us; the launch traced here: 91.7 us
  Pallas kernels  89.7 us (98%)
  between operations  1.36 us (1%)
    pallas_call x2, Pallas kernels, exchange(): pl.pallas_call(functools.partial(exchange_kernel, devices, back, chunks),...  68.3 us
    pallas_call x1, Pallas kernels, shards(): pl.pallas_call(functools.partial(attend_kernel, per_device), out_shape=(j...  12.9 us
    pallas_call x1, Pallas kernels, shards(): pl.pallas_call(functools.partial(gather_kernel, per_device, devices), out...  5.58 us
    pallas_call x1, Pallas kernels, shards(): pl.pallas_call(functools.partial(pick_kernel, per_device, devices), out_s...  2.84 us

profile of v4, /device:TPU:25, one launch (start us, length us, event | category | flops | bytes accessed | tf_op | source)
XLA Modules:
  0.0 91.7 jit_solution(15226462611341704084)
XLA Ops:
  1.3 0.0 copy-start.3
  1.3 0.7 copy-done.3
  2.0 0.0 copy-start
  2.0 0.0 copy-start.1
  2.0 0.0 copy-start.2
  2.0 0.0 copy-start.5
  2.0 2.8 %pick.1 = (bf16[32,2,64,128]{3,2,1,0:T(8,128)(2,1)S(1)}, bf16[2,2,128,512]{3,2,1,0:T(8,128)(2,1)S(1)}) custom-call(s32[1]{0:T(128)} %bitcast.1.me_ref, s32[1]{0:T(128)S(6)} %copy.11.slab_ref, s32[4,8]{1,0:T(4,128)S(1)} %copy-done.3, bf16[16,128,512]{2,1,0:T(8,128)(2,1)} %ck.1, bf16[16,128,512]{2,1,0:T(8,128)(2,1)} %cv.1), custom_call_target="tpu_custom_call" | custom-call | tf_op jit(solution)/shard_map/pick/pallas_call | solution.py:530
  4.8 34.0 %send_out.1 = (bf16[6,2,128,512]{3,2,1,0:T(8,128)(2,1)S(1)}, bf16[4096,128]{1,0:T(8,128)(2,1)S(1)}) custom-call(bf16[2,2,128,512]{3,2,1,0:T(8,128)(2,1)S(1)} %get-tuple-element.14.src, bf16[4096,128]{1,0:T(8,128)(2,1)S(1)} %bitcast.6), custom_call_target="tpu_custom_call" | custom-call | tf_op jit(solution)/shard_map/send_out/pallas_call | solution.py:301
  38.9 0.0 copy-done
  38.9 0.0 copy-done.1
  38.9 0.0 copy-done.2
  38.9 0.0 copy-done.5
  38.9 12.9 %attend.1 = (bf16[128,4096]{1,0:T(8,128)(2,1)}, bf16[6,2,128,512]{3,2,1,0:T(8,128)(2,1)S(1)}, bf16[32,2,64,128]{3,2,1,0:T(8,128)(2,1)S(1)}) custom-call(s32[1]{0:T(128)S(6)} %add.7.first_ref, s32[4,8]{1,0:T(4,128)S(1)} %copy-done.3, s32[4,3]{1,0:T(4,128)S(1)} %copy-done.5, bf16[128,4096]{1,0:T(8,128)(2,1)S(1)} %copy-done, bf16[128,4096]{1,0:T(8,128)(2,1)S(1)} %copy-done.1, ...), custom_call_target="tpu_custom_call" | custom-call | tf_op jit(solution)/shard_map/attend/pallas_call | solution.py:548
  51.8 0.0 copy-start.4
  51.9 34.3 %send_back.1 = (bf16[3,2,128,512]{3,2,1,0:T(8,128)(2,1)S(1)}, bf16[4096,128]{1,0:T(8,128)(2,1)S(1)}) custom-call(bf16[6,2,128,512]{3,2,1,0:T(8,128)(2,1)S(1)} %get-tuple-element.19.src.near, bf16[4096,128]{1,0:T(8,128)(2,1)S(1)} %bitcast.7), custom_call_target="tpu_custom_call" | custom-call | tf_op jit(solution)/shard_map/send_back/pallas_call | solution.py:301
  86.2 0.0 copy-done.4
  86.2 5.6 %assemble.1 = (bf16[16,128,512]{2,1,0:T(8,128)(2,1)}, bf16[16,128,512]{2,1,0:T(8,128)(2,1)}) custom-call(s32[1]{0:T(128)} %bitcast.1.me_ref, s32[1]{0:T(128)S(6)} %copy.11.slab_ref, s32[4,8]{1,0:T(4,128)S(1)} %copy-done.4, bf16[6,2,128,512]{3,2,1,0:T(8,128)(2,1)S(1)} %get-tuple-element.19.src.near, bf16[3,2,128,512]{3,2,1,0:T(8,128)(2,1)S(1)} %get-tuple-element.21.back, ...), custom_call_target="tpu_custom_call" | custom-call | tf_op jit(solution)/shard_map/assemble/pallas_call | solution.py:580
Async XLA Ops:
  1.3 0.7 copy-start.3
  2.0 36.9 %copy-start = (bf16[128,4096]{1,0:T(8,128)(2,1)S(1)}, bf16[128,4096]{1,0:T(8,128)(2,1)}, u32[]{:S(2)}) copy-start(bf16[128,4096]{1,0:T(8,128)(2,1)} %q_ref.1) | copy-start | bytes 3145732
  2.0 36.9 %copy-start.1 = (bf16[128,4096]{1,0:T(8,128)(2,1)S(1)}, bf16[128,4096]{1,0:T(8,128)(2,1)}, u32[]{:S(2)}) copy-start(bf16[128,4096]{1,0:T(8,128)(2,1)} %g_ref.1) | copy-start | bytes 3145732
  2.0 36.9 %copy-start.2 = (bf16[128,4096]{1,0:T(8,128)(2,1)S(1)}, bf16[128,4096]{1,0:T(8,128)(2,1)}, u32[]{:S(2)}) copy-start(bf16[128,4096]{1,0:T(8,128)(2,1)} %f_ref.1) | copy-start | bytes 3145732
  2.0 36.9 %copy-start.5 = (s32[4,3]{1,0:T(4,128)S(1)}, s32[4,3]{1,0:T(4,128)}, u32[]{:S(2)}) copy-start(s32[4,3]{1,0:T(4,128)} %off_ref.1) | copy-start | bytes 148
  51.8 34.3 %copy-start.4 = (s32[4,8]{1,0:T(4,128)S(1)}, s32[4,8]{1,0:T(4,128)}, u32[]{:S(2)}) copy-start(s32[4,8]{1,0:T(4,128)} %vert_ref.5) | copy-start | bytes 388
